TPU v7x, 32 devices: a whole 2x2x4 slice. The times are simulated.
32 devices in a mesh: fsdp: 32 (over z, y, x, core).
Axes of the slice: x: 2, y: 2, z: 4, core: 2. Of those that a mesh axis runs over, the one named last changes fastest.
Arguments:
- inputs: float32 [64, 145, 768], P('fsdp'), may hold values from -6 to 6
- cotangent: float32 [64, 145, 768], P('fsdp'), may hold values from -6 to 6
- counts: int32 [32], P('fsdp'), may hold values from 1 to 2, as said below
- params: float32 [7090176], P('fsdp'), as said below
- moment_one: float32 [7090176], P('fsdp')
- moment_two: float32 [7090176], P('fsdp')
Outputs:
- outputs: float32 [64, 145, 768], P('fsdp')
- input_grad: float32 [64, 145, 768], P('fsdp')
- param_grad: float32 [7090176], P('fsdp')
- new_params: float32 [7090176], P('fsdp')
- new_moment_one: float32 [7090176], P('fsdp')
- new_moment_two: float32 [7090176], P('fsdp')
Inputs may be any that keep to these rules, and one draw needn't show every extreme that they name: `counts`: some device holds 2 images in every draw. `params`: entries past 7087104 are zero.
All inputs are finite; a program needn't handle non-finite values.
Results may differ from a plain program's by a relative error of at most 0.01.
Values may be sent and summed in bfloat16 or wider, within the bound.
No kernel may reach another device: no remote copies, remote signals or barrier semaphores. Data moves between devices by JAX's collectives and lax.ppermute only.
A program may use at most 192 MiB of HBM per device.

v0:
```python
import math

import jax
import jax.numpy as jnp
from jax import lax
from jax.sharding import PartitionSpec as P

D = 768
HD = 64
FF = 3072
PARAMS = 7087104


EPS_NORM = 1e-06
BETA_ONE = 0.9
BETA_TWO = 0.95
RATE = 0.01
DECAY = 0.05
EPS_ADAM = 1e-08
ADAM_STEP = 3.0
INV_ROOT_TWO = 0.7071067811865476
INV_ROOT_TWOPI = 0.3989422804014327


def batched(form, left, right):
    return jnp.einsum(form, left, right, preferred_element_type=jnp.float32)


def unpack(flat):
    layouts = [
        (D,),
        (D,),
        (D, 3 * D),
        (D,),
        (D,),
        (D, D),
        (D,),
        (D,),
        (D,),
        (D, FF),
        (FF,),
        (FF, D),
        (D,),
    ]
    pieces = []
    offset = 0
    for layout_now in layouts:
        number = math.prod(layout_now)
        pieces.append(flat[offset : offset + number].reshape(layout_now))
        offset += number
    return pieces


def layer_norm(values, norm_gain, norm_shift):
    centre = values - jnp.mean(values, axis=-1, keepdims=True)
    scale_inv = lax.rsqrt(jnp.mean(centre * centre, axis=-1, keepdims=True) + EPS_NORM)
    normed = centre * scale_inv
    return (normed * norm_gain + norm_shift, normed, scale_inv)


def norm_back(grad_out, normed, scale_inv, norm_gain):
    gain_grad = jnp.sum(grad_out * normed, axis=(0, 1))
    shift_grad = jnp.sum(grad_out, axis=(0, 1))
    scaled = grad_out * norm_gain
    back = scale_inv * (
        scaled
        - jnp.mean(scaled, axis=-1, keepdims=True)
        - normed * jnp.mean(scaled * normed, axis=-1, keepdims=True)
    )
    return (back, gain_grad, shift_grad)


def run_block(inputs, cotangent, forward_flat, backward_flat, pad_length):
    f32 = jnp.float32
    bf16 = jnp.bfloat16
    (
        norm1_gain,
        norm1_shift,
        qkv_weight,
        query_bias,
        value_bias,
        out_weight,
        out_bias,
        norm2_gain,
        norm2_shift,
        hidden_weight,
        hidden_bias,
        down_weight,
        down_bias,
    ) = unpack(forward_flat)
    image_count, token_count, features = inputs.shape
    row_count = image_count * token_count
    head_count = features // HD
    qk_scale = 1.0 / math.sqrt(HD)
    heads_shape = (image_count, token_count, head_count, HD)
    first_norm, normed_one, inv_one = layer_norm(
        inputs, norm1_gain.astype(f32), norm1_shift.astype(f32)
    )
    act_one = first_norm.reshape(row_count, features).astype(bf16)
    projected = jnp.dot(act_one, qkv_weight, preferred_element_type=f32)
    query_heads = (
        (projected[:, :features] + query_bias.astype(f32)).astype(bf16).reshape(heads_shape)
    )
    key_heads = projected[:, features : 2 * features].astype(bf16).reshape(heads_shape)
    value_heads = (
        (projected[:, 2 * features :] + value_bias.astype(f32)).astype(bf16).reshape(heads_shape)
    )
    scores = batched("sqhd,skhd->shqk", query_heads, key_heads) * qk_scale
    row_max = jnp.max(scores, axis=-1, keepdims=True)
    log_total = row_max + jnp.log(jnp.sum(jnp.exp(scores - row_max), axis=-1, keepdims=True))
    attention = jnp.exp(scores - log_total)
    mixed = batched("shqk,skhd->sqhd", attention.astype(bf16), value_heads)
    mixed_rows = mixed.astype(bf16).reshape(row_count, features)
    attn_out = jnp.dot(mixed_rows, out_weight, preferred_element_type=f32) + out_bias.astype(f32)
    middle = inputs + attn_out.reshape(inputs.shape)
    second_norm, normed_two, inv_two = layer_norm(
        middle, norm2_gain.astype(f32), norm2_shift.astype(f32)
    )
    act_two = second_norm.reshape(row_count, features).astype(bf16)
    pre_act = jnp.dot(act_two, hidden_weight, preferred_element_type=f32) + hidden_bias.astype(f32)
    hidden_rows = jax.nn.gelu(pre_act, approximate=False).astype(bf16)
    outputs = middle + (
        jnp.dot(hidden_rows, down_weight, preferred_element_type=f32) + down_bias.astype(f32)
    ).reshape(inputs.shape)
    (
        norm1_gain,
        norm1_shift,
        qkv_weight,
        query_bias,
        value_bias,
        out_weight,
        out_bias,
        norm2_gain,
        norm2_shift,
        hidden_weight,
        hidden_bias,
        down_weight,
        down_bias,
    ) = unpack(backward_flat)
    grad_rows = cotangent.reshape(row_count, features)
    grad_narrow = grad_rows.astype(bf16)
    grad_down = jnp.dot(hidden_rows.T, grad_narrow, preferred_element_type=f32)
    grad_down_bias = jnp.sum(grad_rows, axis=0)
    slope = (
        0.5 * (1.0 + lax.erf(pre_act * INV_ROOT_TWO))
        + pre_act * jnp.exp(-0.5 * pre_act * pre_act) * INV_ROOT_TWOPI
    )
    d_pre = jnp.dot(grad_narrow, down_weight.T, preferred_element_type=f32) * slope
    d_pre_narrow = d_pre.astype(bf16)
    grad_hidden = jnp.dot(act_two.T, d_pre_narrow, preferred_element_type=f32)
    grad_hidden_bias = jnp.sum(d_pre, axis=0)
    d_act_two = jnp.dot(d_pre_narrow, hidden_weight.T, preferred_element_type=f32).reshape(
        inputs.shape
    )
    d_mid_norm, grad_gain_two, grad_shift_two = norm_back(
        d_act_two, normed_two, inv_two, norm2_gain.astype(f32)
    )
    d_middle = cotangent + d_mid_norm
    d_mid_rows = d_middle.reshape(row_count, features)
    d_mid_narrow = d_mid_rows.astype(bf16)
    grad_out_weight = jnp.dot(mixed_rows.T, d_mid_narrow, preferred_element_type=f32)
    grad_out_bias = jnp.sum(d_mid_rows, axis=0)
    d_mixed = (
        jnp.dot(d_mid_narrow, out_weight.T, preferred_element_type=f32)
        .astype(bf16)
        .reshape(heads_shape)
    )
    scores = batched("sqhd,skhd->shqk", query_heads, key_heads) * qk_scale
    attention = jnp.exp(scores - log_total)
    d_attention = batched("sqhd,skhd->shqk", d_mixed, value_heads)
    row_dot = jnp.sum(attention * d_attention, axis=-1, keepdims=True)
    d_scores = (attention * (d_attention - row_dot) * qk_scale).astype(bf16)
    d_query = batched("shqk,skhd->sqhd", d_scores, key_heads).reshape(row_count, features)
    d_keys = batched("shqk,sqhd->skhd", d_scores, query_heads).reshape(row_count, features)
    d_values = batched("shqk,sqhd->skhd", attention.astype(bf16), d_mixed).reshape(
        row_count, features
    )
    d_proj_narrow = jnp.concatenate([d_query, d_keys, d_values], axis=1).astype(bf16)
    grad_qkv = jnp.dot(act_one.T, d_proj_narrow, preferred_element_type=f32)
    grad_query_bias = jnp.sum(d_query, axis=0)
    grad_value_bias = jnp.sum(d_values, axis=0)
    d_act_one = jnp.dot(d_proj_narrow, qkv_weight.T, preferred_element_type=f32).reshape(
        inputs.shape
    )
    d_in_norm, grad_gain_one, grad_shift_one = norm_back(
        d_act_one, normed_one, inv_one, norm1_gain.astype(f32)
    )
    input_grad = d_middle + d_in_norm
    grads = jnp.concatenate(
        [
            grad_gain_one,
            grad_shift_one,
            grad_qkv.reshape(-1),
            grad_query_bias,
            grad_value_bias,
            grad_out_weight.reshape(-1),
            grad_out_bias,
            grad_gain_two,
            grad_shift_two,
            grad_hidden.reshape(-1),
            grad_hidden_bias,
            grad_down.reshape(-1),
            grad_down_bias,
            jnp.zeros((pad_length,), f32),
        ]
    )
    return (outputs, input_grad, grads)


def adam_update(params, grads, moment_one, moment_two):
    new_one = BETA_ONE * moment_one + (1.0 - BETA_ONE) * grads
    new_two = BETA_TWO * moment_two + (1.0 - BETA_TWO) * grads * grads
    fix_one = 1.0 - BETA_ONE**ADAM_STEP
    fix_two = 1.0 - BETA_TWO**ADAM_STEP
    update = new_one / fix_one / (jnp.sqrt(new_two / fix_two) + EPS_ADAM)
    return (params - RATE * (update + DECAY * params), new_one, new_two)


def local(inputs, cotangent, counts, params, moment_one, moment_two):
    live_slots = (jnp.arange(inputs.shape[0]) < counts[0]).astype(jnp.float32)
    masked = cotangent * live_slots[:, None, None]
    narrow = params.astype(jnp.bfloat16)
    forward_flat = lax.all_gather(narrow, "fsdp", axis=0, tiled=True)
    shard_length = params.shape[0]
    total_length = shard_length * lax.axis_size("fsdp")
    pad_length = total_length - PARAMS
    outputs, input_grad, padded = run_block(inputs, masked, forward_flat, forward_flat, pad_length)
    shard_grad = lax.psum_scatter(padded, "fsdp", scatter_dimension=0, tiled=True)
    new_params, new_one, new_two = adam_update(params, shard_grad, moment_one, moment_two)
    return (outputs, input_grad, shard_grad, new_params, new_one, new_two)


def solution(mesh):
    placed = (
        P("fsdp", None, None),
        P("fsdp", None, None),
        P("fsdp"),
        P("fsdp"),
        P("fsdp"),
        P("fsdp"),
    )
    return jax.shard_map(
        local,
        mesh=mesh,
        in_specs=placed,
        out_specs=(
            P("fsdp", None, None),
            P("fsdp", None, None),
            P("fsdp"),
            P("fsdp"),
            P("fsdp"),
            P("fsdp"),
        ),
        check_vma=False,
    )
```

profile of v0, /device:TPU:0, one launch (start us, length us, event | category | flops | bytes accessed | tf_op | source)
XLA Modules:
  0.0 1364.5 jit_solution(11955516446482131017)
XLA Ops:
  7.2 1.3 convert_element_type.97
  8.6 5.8 reshape.191
  17.4 169.2 %all-gather.3.cloned.1.call-done = bf16[32,1,221568]{2,1,0:T(2,128)(2,1)} async-done(((bf16[1,1,221568]{2,1,0:T(2,128)(2,1)}), bf16[32,1,221568]{2,1,0:T(2,128)(2,1)}) %all-gather.3.cloned.1.call-update) | async-done | bytes 14180368 | tf_op jit(solution)/shard_map/all_gather | solution.py:223
  186.6 255.5 %reduce.4 = bf16[32,221568]{1,0:T(8,128)(2,1)} reduce(bf16[32,1,221568]{2,1,0:T(2,128)(2,1)} %all-gather.3.cloned.1.call-done, bf16[]{:T(256)} %constant.106), dimensions={1}, to_apply=%all-gather.reduce_sub_computation | reduce | bytes 28360706 | tf_op jit(solution)/shard_map/all_gather | solution.py:223
  442.1 24.9 %reshape.192 = bf16[7090176]{0:T(1024)(128)(2,1)} reshape(bf16[32,221568]{1,0:T(8,128)(2,1)} %reduce.4) | data formatting | bytes 28360704
  467.1 1.4 slice_convert_fusion.2
  468.5 2.4 slice.95
  470.9 1.3 slice_convert_fusion.1
  472.2 9.7 fusion.71
  481.9 8.2 reshape.181
  490.1 8.2 reshape.193
  498.3 5.2 reshape.175
  503.6 5.2 reshape.194
  508.8 1.4 add_convert_fusion.1
  510.3 3.4 fusion.75
  518.0 1.7 copy.140
  519.6 1.9 multiply_reduce_fusion.1
  524.6 2.0 slice.84
  526.7 2.8 convolution_add_fusion.1
  532.2 9.4 slice.91
  541.7 11.8 fusion.4
  553.5 4.2 fusion.72
  557.6 3.1 dot_general.64
  560.7 5.4 convolution_add_fusion.2
  567.4 5.6 multiply_reduce_fusion.2
  573.0 2.0 fusion.69
  576.1 2.0 convolution_convert_fusion.1
  578.1 1.7 reshape.200
  579.8 2.1 copy.147
  581.9 4.3 bitcast_convert_fusion
  586.2 2.6 fusion.76
  588.9 8.4 fusion.45
  597.2 8.9 bitcast_convert_fusion.1
  606.2 2.1 fusion.77
  608.3 5.1 convolution_bitcast_fusion
  613.4 5.0 fusion.78
  618.5 1.7 copy.160
  620.2 2.1 copy.157
  622.3 2.2 copy.156
  624.5 2.8 copy.158
  627.3 2.1 copy.155
  629.4 3.5 reshape.186
  633.0 2.8 copy.159
  635.8 3.1 reshape.185
  638.9 3.1 reshape.184
  642.0 6.5 fusion.33
  648.5 7.9 reshape.187
  656.4 1.6 bitcast_reduce_fusion.1
  658.1 1.6 bitcast_reduce_fusion
  659.8 1.6 reshape.188
  661.4 9.5 copy.175
  670.8 10.9 reshape.190
  681.7 4.3 multiply_reduce_fusion.3
  688.7 60.9 %dynamic-update-slice.2 = f32[7090176]{0:T(1024)} dynamic-update-slice(f32[7090176]{0:T(1024)} %constant_dynamic-update-slice_fusion.8, f32[1769472]{0:T(1024)} %reshape.187, s32[]{} %constant.109) | dynamic-update-slice | bytes 14155780
  752.1 1.6 constant_dynamic-update-slice_fusion.5
  757.6 80.6 %dynamic-update-slice.9 = f32[7090176]{0:T(1024)} dynamic-update-slice(f32[7090176]{0:T(1024)} %constant_dynamic-update-slice_fusion.2, f32[2359296]{0:T(1024)} %bitcast.56, s32[]{} %constant.116) | dynamic-update-slice | bytes 18874372
  838.2 1.3 constant_dynamic-update-slice_fusion.1
  839.5 80.3 %dynamic-update-slice.11 = f32[7090176]{0:T(1024)} dynamic-update-slice(f32[7090176]{0:T(1024)} %constant_dynamic-update-slice_fusion.1, f32[2359296]{0:T(1024)} %reshape.190, s32[]{} %constant.118) | dynamic-update-slice | bytes 18874372
  919.8 1.3 constant_dynamic-update-slice_fusion
  922.9 1.4 copy.161
  924.3 1.7 multiply_add_fusion
  926.0 1.4 copy.162
  927.4 425.8 %all-reduce.3.cloned.1.call-done = f32[7090176]{0:T(1024)} async-done(((f32[7090176]{0:T(1024)}), f32[7090176]{0:T(1024)}) %all-reduce.3.cloned.1.call-update) | async-done | bytes 28360720
  1353.2 4.3 multiply_subtract_fusion
  (151 shorter events, 25.7 us)
Async XLA Ops:
  7.2 7.3 copy-start.1
  7.2 8.9 copy-start.10
  7.2 179.4 %all-gather.3.cloned.1.call-start = ((), (), s32[]{:S(2)}) async-start(), calls=%async_computation | async-start | bytes 29246976 | tf_op jit(solution)/shard_map/all_gather | solution.py:223
  14.4 1338.8 %all-reduce.3.cloned.1.call-start = ((), (), s32[]{:S(2)}) async-start(), calls=%async_computation.1 | async-start | bytes 56721408
  15.5 0.5 copy-start.48
  17.1 491.7 %copy-start.29 = (f32[2,145]{1,0:T(2,128)}, f32[2,145]{1,0:T(2,128)S(1)}, u32[]{:S(2)}) copy-start(f32[2,145]{1,0:T(2,128)S(1)} %broadcast_multiply_fusion.5) | copy-start | bytes 3484
  17.4 491.4 %copy-start.33 = (f32[2,145]{1,0:T(2,128)}, f32[2,145]{1,0:T(2,128)S(1)}, u32[]{:S(2)}) copy-start(f32[2,145]{1,0:T(2,128)S(1)} %add_rsqrt_fusion.1) | copy-start | bytes 3484
  510.2 3.5 copy-start.20
  510.3 3.5 copy-start.38
  510.3 3.5 copy-start.39
  517.2 4.3 copy-start.13
  521.5 1.8 copy-start
  522.3 1.1 copy-start.27
  522.3 2.3 slice-start
  523.4 3.3 copy-start.45
  524.6 4.9 copy-start.17
  526.7 4.1 copy-start.2
  530.8 1.1 copy-start.37
  531.0 0.6 copy-start.31
  531.3 0.6 copy-start.35
  532.2 9.4 copy-start.21
  532.2 9.4 copy-start.43
  541.7 11.8 copy-start.8
  541.7 11.8 copy-start.18
  557.6 3.1 copy-start.44
  567.4 5.6 copy-start.11
  567.4 5.6 copy-start.32
  567.4 5.6 copy-start.36
  567.4 5.6 copy-start.49
  575.0 0.9 copy-start.4
  576.0 6.0 copy-start.28
  576.1 2.0 copy-start.23
  586.2 2.6 copy-start.14
  588.8 8.4 copy-start.15
  606.2 2.1 copy-start.6
  606.2 2.1 copy-start.22
  608.3 5.1 copy-start.16
  608.3 5.1 copy-start.19
  613.4 5.0 copy-start.7
  670.8 10.9 copy-start.24
  670.8 10.9 copy-start.25
  670.8 10.9 copy-start.26
  670.8 10.9 copy-start.30
  670.8 10.9 copy-start.34
  688.7 63.5 %copy-start.3 = (f32[589824]{0:T(1024)S(1)}, f32[589824]{0:T(1024)}, u32[]{:S(2)}) copy-start(f32[589824]{0:T(1024)} %reshape.188) | copy-start | bytes 7077892
  749.6 4.2 copy-start.41
  749.6 5.5 copy-start.47
  749.6 6.8 copy-start.46
  757.6 80.6 %copy-start.42 = (f32[3072]{0:T(1024)S(1)}, f32[3072]{0:T(1024)}, u32[]{:S(2)}) copy-start(f32[3072]{0:T(1024)} %get-tuple-element.62) | copy-start | bytes 36868
  839.5 80.3 %copy-start.40 = (f32[768]{0:T(1024)S(1)}, f32[768]{0:T(1024)}, u32[]{:S(2)}) copy-start(f32[768]{0:T(1024)} %get-tuple-element.67) | copy-start | bytes 9220
  921.7 1.2 copy-start.9
  921.7 2.6 copy-start.5
  924.3 428.9 %copy-start.12 = (f32[221568]{0:T(1024)S(1)}, f32[221568]{0:T(1024)}, u32[]{:S(2)}) copy-start(f32[221568]{0:T(1024)} %param.9) | copy-start | bytes 2658820
Sparse Core Ops, SparseCore 0:
  14.5 172.0 all-gather.2
  921.8 431.2 all-reduce.2
where the time goes:
time: 1390 us; the launch traced here: 1360 us
  waiting for transfers between devices  595 us (43%)
  local copies, waits for them, and re-layouts  394 us (28%)
  other arithmetic  274 us (20%)
  matrix products  85.2 us (6%)
  between operations  15.5 us (1%)
    unnamed x3, waiting for transfers between devices  426 us
    unnamed x118, local copies, waits for them, and re-layouts  281 us
    all_gather x1, other arithmetic, local(): forward_flat = lax.all_gather(narrow, 'fsdp', axis=0, tiled=True)  256 us
    all_gather x1, waiting for transfers between devices, local(): forward_flat = lax.all_gather(narrow, 'fsdp', axis=0, tiled=True)  169 us
  transfers between devices with their start and end apart: 2, of which 2 were waited for; matrix products, arithmetic and copies ran while one was open for 0% of the time, Pallas kernels for 0%

commit v1 on v0

v1 whole, which is shorter than its diff:
```python
import functools
import math

import jax
import jax.numpy as jnp
from jax import lax
from jax.experimental import pallas as pl
from jax.experimental.pallas import tpu as pltpu
from jax.sharding import PartitionSpec as P

D = 768
HD = 64
FF = 3072
PARAMS = 7087104
LANES = 128
TPAD = 384

EPS_NORM = 1e-06
BETA_ONE = 0.9
BETA_TWO = 0.95
RATE = 0.01
DECAY = 0.05
EPS_ADAM = 1e-08
ADAM_STEP = 3.0
INV_ROOT_TWO = 0.7071067811865476
INV_ROOT_TWOPI = 0.3989422804014327
F32 = jnp.float32
BF16 = jnp.bfloat16

SEGMENTS = (
    ("g1", 1, 6),
    ("c1", 1, 6),
    ("wqkv", D, 18),
    ("bq", 1, 6),
    ("bv", 1, 6),
    ("wo", D, 6),
    ("bo", 1, 6),
    ("g2", 1, 6),
    ("c2", 1, 6),
    ("w1", D, 24),
    ("b1", 1, 24),
    ("w2", FF, 6),
    ("b2", 1, 6),
)
GROUPS = (("g1", "c1", "wqkv", "bq", "bv"), ("wo", "bo", "g2", "c2"), ("w1", "b1"), ("w2", "b2"))
OFFSETS = {}
SHAPES = {}
_at = 0
for _name, _k, _j in SEGMENTS:
    OFFSETS[_name] = _at
    SHAPES[_name] = (_k, _j)
    _at += _k * _j
USED_ROWS = _at


def round_up(value, step):
    return -(-value // step) * step


class Plan:
    def __init__(self, devices, shard):
        self.devices = devices
        self.bits = devices.bit_length() - 1
        self.rows = shard // LANES
        self.padded = round_up(self.rows, 16)
        half = round_up(self.padded // 2, 16)
        self.halves = ((0, half), (half, self.padded))
        self.quarters = 4
        self.low = devices // self.quarters
        self.low_bits = self.bits - 2

    def low_order(self, half):
        order = [1, 2] if half == 0 else [2, 1]
        return list(range(self.low_bits - 1, 2, -1)) + order + [0]


def exchange(array, mask, devices):
    return lax.ppermute(array, "fsdp", [(i, i ^ mask) for i in range(devices)])


def gather_quarters(narrow, plan, me):
    quarter = me // plan.low
    result = [[None, None] for _ in range(plan.quarters)]
    for half, (lo, hi) in enumerate(plan.halves):
        part = narrow[None, None, lo:hi]
        for axis, bit in ((0, plan.bits - 1), (1, plan.bits - 2)):
            part = jnp.concatenate([part, exchange(part, 1 << bit, plan.devices)], axis=axis)
        part = part.reshape((plan.quarters,) + part.shape[2:])
        for q in range(plan.quarters):
            block = lax.dynamic_index_in_dim(part, quarter ^ q, 0, keepdims=False)
            block = block.reshape((1,) * plan.low_bits + block.shape)
            for bit in plan.low_order(half):
                axis = plan.low_bits - 1 - bit
                block = jnp.concatenate([block, exchange(block, 1 << bit, plan.devices)], axis=axis)
            result[q][half] = block.reshape((plan.low,) + block.shape[-2:])
    return result


def unpack_group(names, gathered, plan, position):
    start = OFFSETS[names[0]]
    stop = OFFSETS[names[-1]] + math.prod(SHAPES[names[-1]])
    first, last = start // plan.rows, (stop - 1) // plan.rows
    count = last - first + 1
    quarters = list(range(first // plan.low, last // plan.low + 1))
    flat_rows = round_up(stop - start, 8) + 8

    def kernel(*refs):
        position_ref = refs[0]
        sources = refs[1 : 1 + 2 * len(quarters)]
        outs = refs[1 + 2 * len(quarters) : -3]
        stage, flat, sems = refs[-3:]
        mine = position_ref[0]
        copies = []
        for i in range(count):
            device = first + i
            q = device // plan.low - quarters[0]
            spot = (device % plan.low) ^ mine
            for half, (lo, hi) in enumerate(plan.halves):
                copy = pltpu.make_async_copy(
                    sources[2 * q + half].at[spot], stage.at[i, lo:hi], sems.at[i, half]
                )
                copy.start()
                copies.append(copy)
        for i in range(count):
            copies[2 * i].wait()
            copies[2 * i + 1].wait()
            base = (first + i) * plan.rows
            row = max(start, base)
            end = min(stop, base + plan.rows)
            while row < end:
                inside = row - base
                lower = inside // 16 * 16
                upper = min(lower + 256, end - base)
                block = stage[i, lower : round_up(upper, 16), :].astype(F32)
                flat[row - start : base + upper - start, :] = block[inside - lower : upper - lower]
                row = base + upper
        for name, out in zip(names, outs):
            rows, blocks = SHAPES[name]
            offset = OFFSETS[name] - start
            if rows == 1:
                for j in range(blocks):
                    out[:, j * LANES : (j + 1) * LANES] = flat[offset + j : offset + j + 1, :]
            else:

                @pl.loop(0, blocks)
                def _(j, out=out, rows=rows, blocks=blocks, offset=offset):
                    column = flat[pl.ds(offset + j, rows, stride=blocks), :]
                    out[:, pl.ds(pl.multiple_of(j * LANES, LANES), LANES)] = column.astype(BF16)

    shapes = []
    for name in names:
        rows, blocks = SHAPES[name]
        kind = F32 if rows == 1 else BF16
        shapes.append(jax.ShapeDtypeStruct((rows, blocks * LANES), kind))
    operands = [gathered[q][half] for q in quarters for half in range(2)]
    results = pl.pallas_call(
        kernel,
        out_shape=shapes,
        in_specs=[pl.BlockSpec(memory_space=pltpu.SMEM)]
        + [pl.BlockSpec(memory_space=pl.ANY)] * len(operands),
        out_specs=[pl.BlockSpec(memory_space=pltpu.VMEM)] * len(shapes),
        scratch_shapes=[
            pltpu.VMEM((count, plan.padded, LANES), BF16),
            pltpu.VMEM((flat_rows, LANES), F32),
            pltpu.SemaphoreType.DMA((count, 2)),
        ],
        cost_estimate=pl.CostEstimate(
            flops=0, bytes_accessed=4 * (stop - start) * LANES, transcendentals=0
        ),
        name="unpack_" + names[0],
    )(position, *operands)
    return dict(zip(names, results))


def pack_quarter(quarter, factors, vectors, plan):
    start = quarter * plan.low * plan.rows
    stop = start + plan.low * plan.rows
    pieces = []
    base, top = start, stop
    for name, rows, blocks in SEGMENTS:
        offset = OFFSETS[name]
        lo, hi = max(start, offset), min(stop, offset + rows * blocks)
        if lo >= hi:
            continue
        if rows == 1:
            pieces.append((name, offset, lo - offset, hi - offset))
        else:
            k0 = (lo - offset) // blocks // LANES * LANES
            k1 = round_up(-(-(hi - offset) // blocks), LANES)
            pieces.append((name, offset, k0, k1))
            base = min(base, offset + k0 * blocks)
            top = max(top, offset + k1 * blocks)
    flat_rows = round_up(top - base, 8) + 32
    operands = []
    for name, *_ in pieces:
        operands.extend(factors[name] if name in factors else (vectors[name],))

    def kernel(*refs):
        ins = list(refs[: len(operands)])
        outs = refs[len(operands) : len(operands) + 2]
        flat, turned = refs[len(operands) + 2 :]
        for name, offset, lo, hi in pieces:
            rows, blocks = SHAPES[name]
            if rows == 1:
                row_ref = ins.pop(0)
                for j in range(lo, hi):
                    at = offset + j - base
                    flat[at : at + 1, :] = row_ref[:, j * LANES : (j + 1) * LANES]
                continue
            left, right = ins.pop(0), ins.pop(0)
            size = hi - lo
            step = 256 if size % 256 == 0 else 128
            for k in range(lo, hi, 128):
                turned[k - lo : k - lo + 128, :] = left[:, k : k + 128].T

            @pl.loop(0, blocks // 2)
            def _(pair, right=right, lo=lo, size=size, step=step, offset=offset, blocks=blocks):
                columns = right[:, pl.ds(pl.multiple_of(pair * 256, 256), 256)]

                @pl.loop(0, size // step)
                def _(part):
                    k = pl.multiple_of(part * step, step)
                    product = jnp.dot(
                        turned[pl.ds(k, step), :], columns, preferred_element_type=F32
                    )
                    at = offset - base + (lo + k) * blocks + 2 * pair
                    flat[pl.ds(at, step, stride=blocks), :] = product[:, :LANES]
                    flat[pl.ds(at + 1, step, stride=blocks), :] = product[:, LANES:]

        if stop > USED_ROWS:
            flat[max(start, USED_ROWS) - base : stop - base, :] = jnp.zeros(
                (stop - max(start, USED_ROWS), LANES), F32
            )
        for i in range(plan.low):
            for (lo, hi), out in zip(plan.halves, outs):
                for row in range(lo, hi, 256):
                    end = min(row + 256, hi)
                    at = start - base + i * plan.rows
                    out[i, row - lo : end - lo, :] = flat[at + row : at + end, :].astype(BF16)

    widest = max([hi - lo for name, _, lo, hi in pieces if SHAPES[name][0] > 1] + [128])
    return pl.pallas_call(
        kernel,
        out_shape=[
            jax.ShapeDtypeStruct((plan.low, hi - lo, LANES), BF16) for lo, hi in plan.halves
        ],
        in_specs=[pl.BlockSpec(memory_space=pltpu.VMEM)] * len(operands),
        out_specs=[pl.BlockSpec(memory_space=pltpu.VMEM)] * 2,
        scratch_shapes=[pltpu.VMEM((flat_rows, LANES), F32), pltpu.VMEM((widest, TPAD), BF16)],
        cost_estimate=pl.CostEstimate(
            flops=2 * (top - base) * LANES * TPAD,
            bytes_accessed=4 * (top - base) * LANES,
            transcendentals=0,
        ),
        name=f"pack_{quarter}",
    )(*operands)


def halve(array, axis, bit, plan, me, last=False):
    mine = (me >> bit) & 1
    keep = lax.dynamic_index_in_dim(array, mine, axis, keepdims=False)
    send = lax.dynamic_index_in_dim(array, 1 - mine, axis, keepdims=False)
    total = keep.astype(F32) + exchange(send, 1 << bit, plan.devices).astype(F32)
    return total if last else total.astype(BF16)


def scatter_quarters(packed, plan, me):
    parts = []
    for half in range(2):
        blocks = []
        for q in range(plan.quarters):
            block = packed[q][half]
            block = block.reshape((2,) * plan.low_bits + block.shape[1:])
            left = list(range(plan.low_bits - 1, -1, -1))
            for bit in reversed(plan.low_order(half)):
                block = halve(block, left.index(bit), bit, plan, me)
                left.remove(bit)
            blocks.append(block)
        stacked = jnp.stack(blocks).reshape((2, 2) + blocks[0].shape)
        stacked = halve(stacked, 1, plan.bits - 2, plan, me)
        parts.append(halve(stacked, 0, plan.bits - 1, plan, me, last=True))
    return jnp.concatenate(parts, axis=0)[: plan.rows]


def batched(form, left, right):
    return jnp.einsum(form, left, right, preferred_element_type=F32)


def layer_norm(values, norm_gain, norm_shift):
    centre = values - jnp.mean(values, axis=-1, keepdims=True)
    scale_inv = lax.rsqrt(jnp.mean(centre * centre, axis=-1, keepdims=True) + EPS_NORM)
    normed = centre * scale_inv
    return (normed * norm_gain + norm_shift, normed, scale_inv)


def norm_back(grad_out, normed, scale_inv, norm_gain):
    gain_grad = jnp.sum(grad_out * normed, axis=(0, 1))
    shift_grad = jnp.sum(grad_out, axis=(0, 1))
    scaled = grad_out * norm_gain
    back = scale_inv * (
        scaled
        - jnp.mean(scaled, axis=-1, keepdims=True)
        - normed * jnp.mean(scaled * normed, axis=-1, keepdims=True)
    )
    return (back, gain_grad, shift_grad)


def run_block(inputs, cotangent, w):
    image_count, token_count, features = inputs.shape
    row_count = image_count * token_count
    head_count = features // HD
    qk_scale = 1.0 / math.sqrt(HD)
    heads_shape = (image_count, token_count, head_count, HD)
    first_norm, normed_one, inv_one = layer_norm(inputs, w["g1"], w["c1"])
    act_one = first_norm.reshape(row_count, features).astype(BF16)
    projected = jnp.dot(act_one, w["wqkv"], preferred_element_type=F32)
    query_heads = (projected[:, :features] + w["bq"]).astype(BF16).reshape(heads_shape)
    key_heads = projected[:, features : 2 * features].astype(BF16).reshape(heads_shape)
    value_heads = (projected[:, 2 * features :] + w["bv"]).astype(BF16).reshape(heads_shape)
    scores = batched("sqhd,skhd->shqk", query_heads, key_heads) * qk_scale
    row_max = jnp.max(scores, axis=-1, keepdims=True)
    log_total = row_max + jnp.log(jnp.sum(jnp.exp(scores - row_max), axis=-1, keepdims=True))
    attention = jnp.exp(scores - log_total)
    mixed = batched("shqk,skhd->sqhd", attention.astype(BF16), value_heads)
    mixed_rows = mixed.astype(BF16).reshape(row_count, features)
    attn_out = jnp.dot(mixed_rows, w["wo"], preferred_element_type=F32) + w["bo"]
    middle = inputs + attn_out.reshape(inputs.shape)
    second_norm, normed_two, inv_two = layer_norm(middle, w["g2"], w["c2"])
    act_two = second_norm.reshape(row_count, features).astype(BF16)
    pre_act = jnp.dot(act_two, w["w1"], preferred_element_type=F32) + w["b1"]
    hidden_rows = jax.nn.gelu(pre_act, approximate=False).astype(BF16)
    outputs = middle + (
        jnp.dot(hidden_rows, w["w2"], preferred_element_type=F32) + w["b2"]
    ).reshape(inputs.shape)
    grad_rows = cotangent.reshape(row_count, features)
    grad_narrow = grad_rows.astype(BF16)
    slope = (
        0.5 * (1.0 + lax.erf(pre_act * INV_ROOT_TWO))
        + pre_act * jnp.exp(-0.5 * pre_act * pre_act) * INV_ROOT_TWOPI
    )
    d_pre = jnp.dot(grad_narrow, w["w2"].T, preferred_element_type=F32) * slope
    d_pre_narrow = d_pre.astype(BF16)
    d_act_two = jnp.dot(d_pre_narrow, w["w1"].T, preferred_element_type=F32).reshape(inputs.shape)
    d_mid_norm, grad_gain_two, grad_shift_two = norm_back(d_act_two, normed_two, inv_two, w["g2"])
    d_middle = cotangent + d_mid_norm
    d_mid_rows = d_middle.reshape(row_count, features)
    d_mid_narrow = d_mid_rows.astype(BF16)
    d_mixed = (
        jnp.dot(d_mid_narrow, w["wo"].T, preferred_element_type=F32)
        .astype(BF16)
        .reshape(heads_shape)
    )
    d_attention = batched("sqhd,skhd->shqk", d_mixed, value_heads)
    row_dot = jnp.sum(attention * d_attention, axis=-1, keepdims=True)
    d_scores = (attention * (d_attention - row_dot) * qk_scale).astype(BF16)
    d_query = batched("shqk,skhd->sqhd", d_scores, key_heads).reshape(row_count, features)
    d_keys = batched("shqk,sqhd->skhd", d_scores, query_heads).reshape(row_count, features)
    d_values = batched("shqk,sqhd->skhd", attention.astype(BF16), d_mixed).reshape(
        row_count, features
    )
    d_proj_narrow = jnp.concatenate([d_query, d_keys, d_values], axis=1).astype(BF16)
    d_act_one = jnp.dot(d_proj_narrow, w["wqkv"].T, preferred_element_type=F32).reshape(
        inputs.shape
    )
    d_in_norm, grad_gain_one, grad_shift_one = norm_back(d_act_one, normed_one, inv_one, w["g1"])
    input_grad = d_middle + d_in_norm
    pad = lambda rows: jnp.pad(rows, ((0, TPAD - row_count), (0, 0)))
    factors = {
        "wqkv": (pad(act_one), pad(d_proj_narrow)),
        "wo": (pad(mixed_rows), pad(d_mid_narrow)),
        "w1": (pad(act_two), pad(d_pre_narrow)),
        "w2": (pad(hidden_rows), pad(grad_narrow)),
    }
    vectors = {
        "g1": grad_gain_one,
        "c1": grad_shift_one,
        "bq": jnp.sum(d_query, axis=0),
        "bv": jnp.sum(d_values, axis=0),
        "bo": jnp.sum(d_mid_rows, axis=0),
        "g2": grad_gain_two,
        "c2": grad_shift_two,
        "b1": jnp.sum(d_pre, axis=0),
        "b2": jnp.sum(grad_rows, axis=0),
    }
    vectors = {name: value.reshape(1, -1) for name, value in vectors.items()}
    return (outputs, input_grad, factors, vectors)


def adam_update(params, grads, moment_one, moment_two):
    new_one = BETA_ONE * moment_one + (1.0 - BETA_ONE) * grads
    new_two = BETA_TWO * moment_two + (1.0 - BETA_TWO) * grads * grads
    fix_one = 1.0 - BETA_ONE**ADAM_STEP
    fix_two = 1.0 - BETA_TWO**ADAM_STEP
    update = new_one / fix_one / (jnp.sqrt(new_two / fix_two) + EPS_ADAM)
    return (params - RATE * (update + DECAY * params), new_one, new_two)


def local(plan, inputs, cotangent, counts, params, moment_one, moment_two):
    me = lax.axis_index("fsdp")
    live_slots = (jnp.arange(inputs.shape[0]) < counts[0]).astype(F32)
    masked = cotangent * live_slots[:, None, None]
    rows = params.reshape(plan.rows, LANES)
    narrow = jnp.pad(rows.astype(BF16), ((0, plan.padded - plan.rows), (0, 0)))
    gathered = gather_quarters(narrow, plan, me)
    position = (me % plan.low).astype(jnp.int32).reshape(1)
    weights = {}
    for names in GROUPS:
        weights.update(unpack_group(names, gathered, plan, position))
    outputs, input_grad, factors, vectors = run_block(inputs, masked, weights)
    packed = [pack_quarter(q, factors, vectors, plan) for q in range(plan.quarters)]
    shard_grad = scatter_quarters(packed, plan, me)
    new_params, new_one, new_two = adam_update(
        rows,
        shard_grad,
        moment_one.reshape(plan.rows, LANES),
        moment_two.reshape(plan.rows, LANES),
    )
    flat = lambda array: array.reshape(-1)
    return (outputs, input_grad, flat(shard_grad), flat(new_params), flat(new_one), flat(new_two))


def solution(mesh):
    devices = mesh.shape["fsdp"]

    def step(inputs, cotangent, counts, params, moment_one, moment_two):
        plan = Plan(devices, params.shape[0] // devices)
        placed = (P("fsdp", None, None),) * 2 + (P("fsdp"),) * 4
        return jax.shard_map(
            functools.partial(local, plan),
            mesh=mesh,
            in_specs=placed,
            out_specs=placed,
            check_vma=False,
        )(inputs, cotangent, counts, params, moment_one, moment_two)

    return step
```

time: 1390 us -> 464 us (0.33); the launches traced: 1360 us -> 458 us
  waiting for transfers between devices: 595 us -> 159 us
  local copies, waits for them, and re-layouts: 394 us -> 63 us
  other arithmetic: 274 us -> 47.7 us
  Pallas kernels: 0 us -> 71.9 us
  starting transfers between devices: 0.08 us -> 52 us
  matrix products: 85.2 us -> 60.8 us
    unnamed x3 -> x0, waiting for transfers between devices: 426 us -> none
    unnamed x118 -> x112, local copies, waits for them, and re-layouts: 281 us -> 6.21 us
    all_gather x1 -> x0, other arithmetic: 256 us -> none  [local(): forward_flat = lax.all_gather(narrow, 'fsdp', axis=0, tiled=True)]
    all_gather x1 -> x0, waiting for transfers between devices: 169 us -> none  [local(): forward_flat = lax.all_gather(narrow, 'fsdp', axis=0, tiled=True)]
    ppermute x0 -> x56, waiting for transfers between devices: none -> 159 us  [exchange(): return lax.ppermute(array, 'fsdp', [(i, i ^ mask) for i in range(devices)])]
    pallas_call x0 -> x8, Pallas kernels: none -> 71.9 us  [the longest x4 50.7 us: pack_quarter(): pl.pallas_call(kernel, out_shape=[jax.ShapeDtypeStruct((plan.low, hi - lo...]
    ppermute x0 -> x56, starting transfers between devices: none -> 52 us  [exchange(): return lax.ppermute(array, 'fsdp', [(i, i ^ mask) for i in range(devices)])]
    reshape x18 -> x25, local copies, waits for them, and re-layouts: 61.9 us -> 23.6 us  [the longest x8 4.81 us: run_block(): vectors = {name: value.reshape(1, -1) for name, value in vectors.items()}]
  transfers between devices with their start and end apart: 2 -> 56, of which waited for: 2 -> 26; matrix products, arithmetic and copies ran while one was open for 0% -> 10% of each run, Pallas kernels for 0% -> 12%
where the time goes in v1:
time: 464 us; the launch traced here: 458 us
  waiting for transfers between devices  159 us (34%)
  Pallas kernels  71.9 us (15%)
  local copies, waits for them, and re-layouts  63 us (14%)
  matrix products  60.8 us (13%)
  starting transfers between devices  52 us (11%)
  other arithmetic  47.7 us (10%)
    ppermute x56, waiting for transfers between devices, exchange(): return lax.ppermute(array, 'fsdp', [(i, i ^ mask) for i in range(devices)])  159 us
    ppermute x56, starting transfers between devices, exchange(): return lax.ppermute(array, 'fsdp', [(i, i ^ mask) for i in range(devices)])  52 us
    pallas_call x4, Pallas kernels, pack_quarter(): pl.pallas_call(kernel, out_shape=[jax.ShapeDtypeStruct((plan.low, hi - lo...  50.7 us
    dot_general x6, matrix products, batched(): return jnp.einsum(form, left, right, preferred_element_type=F32)  26.9 us
    pallas_call x4, Pallas kernels, unpack_group(): pl.pallas_call(kernel, out_shape=shapes, in_specs=[pl.BlockSpec(memory_sp...  21.2 us
    concatenate x24, other arithmetic, gather_quarters(): jnp.concatenate([block, exchange(block, 1 << bit, plan.devices)], axis=axis)  19 us
    dot_general x1, matrix products, run_block(): pre_act = jnp.dot(act_two, w['w1'], preferred_element_type=F32) + w['b1']  11.1 us
  transfers between devices with their start and end apart: 56, of which 26 were waited for; matrix products, arithmetic and copies ran while one was open for 10% of the time, Pallas kernels for 12%

profile of v1, /device:TPU:0, one launch (start us, length us, event | category | flops | bytes accessed | tf_op | source)
XLA Modules:
  0.0 457.9 jit_solution(3748412206599329904)
XLA Ops:
  2.0 4.1 collective-permute-start.5
  9.8 12.3 %collective-permute-done.5 = bf16[1,1,864,128]{3,2,1,0:T(8,128)(2,1)S(1)} collective-permute-done((bf16[1,1,864,128]{3,2,1,0:T(8,128)(2,1)S(1)}, bf16[1,1,864,128]{3,2,1,0:T(8,128)(2,1)S(1)}, u32[]{:S(2)}, u32[]{:S(2)}) %collective-permute-start.5) | collective-permute-done | bytes 221216 | tf_op jit(solution)/shard_map/ppermute | solution.py:78
  22.4 3.7 collective-permute-done
  26.9 8.7 %collective-permute-done.6 = bf16[2,1,864,128]{3,2,1,0:T(8,128)(2,1)S(1)} collective-permute-done((bf16[2,1,864,128]{3,2,1,0:T(8,128)(2,1)S(1)}, bf16[2,1,864,128]{3,2,1,0:T(8,128)(2,1)S(1)}, u32[]{:S(2)}, u32[]{:S(2)}) %collective-permute-start.6) | collective-permute-done | bytes 442400 | tf_op jit(solution)/shard_map/ppermute | solution.py:78
  35.7 1.6 collective-permute-start.25
  39.9 5.3 %collective-permute-done.1 = bf16[2,1,880,128]{3,2,1,0:T(8,128)(2,1)S(1)} collective-permute-done((bf16[2,1,880,128]{3,2,1,0:T(8,128)(2,1)S(1)}, bf16[2,1,880,128]{3,2,1,0:T(8,128)(2,1)S(1)}, u32[]{:S(2)}, u32[]{:S(2)}) %collective-permute-start.1) | collective-permute-done | bytes 450592 | tf_op jit(solution)/shard_map/ppermute | solution.py:78
  46.9 10.4 %collective-permute-done.7 = bf16[1,1,1,864,128]{4,3,2,1,0:T(8,128)(2,1)S(1)} collective-permute-done((bf16[1,1,1,864,128]{4,3,2,1,0:T(8,128)(2,1)S(1)}, bf16[1,1,1,864,128]{4,3,2,1,0:T(8,128)(2,1)S(1)}, u32[]{:S(2)}, u32[]{:S(2)}) %collective-permute-start.7) | collective-permute-done | bytes 221216 | tf_op jit(solution)/shard_map/ppermute | solution.py:78
  61.7 13.6 %collective-permute-done.2 = bf16[1,1,1,880,128]{4,3,2,1,0:T(8,128)(2,1)S(1)} collective-permute-done((bf16[1,1,1,880,128]{4,3,2,1,0:T(8,128)(2,1)S(1)}, bf16[1,1,1,880,128]{4,3,2,1,0:T(8,128)(2,1)S(1)}, u32[]{:S(2)}, u32[]{:S(2)}) %collective-permute-start.2) | collective-permute-done | bytes 225312 | tf_op jit(solution)/shard_map/ppermute | solution.py:78
  80.7 4.1 collective-permute-done.26
  86.4 7.9 %collective-permute-done.20 = bf16[2,1,1,864,128]{4,3,2,1,0:T(8,128)(2,1)S(1)} collective-permute-done((bf16[2,1,1,864,128]{4,3,2,1,0:T(8,128)(2,1)S(1)}, bf16[2,1,1,864,128]{4,3,2,1,0:T(8,128)(2,1)S(1)}, u32[]{:S(2)}, u32[]{:S(2)}) %collective-permute-start.20) | collective-permute-done | bytes 442400 | tf_op jit(solution)/shard_map/ppermute | solution.py:78
  95.9 7.8 %collective-permute-done.14 = bf16[2,1,1,864,128]{4,3,2,1,0:T(8,128)(2,1)S(1)} collective-permute-done((bf16[2,1,1,864,128]{4,3,2,1,0:T(8,128)(2,1)S(1)}, bf16[2,1,1,864,128]{4,3,2,1,0:T(8,128)(2,1)S(1)}, u32[]{:S(2)}, u32[]{:S(2)}) %collective-permute-start.14) | collective-permute-done | bytes 442400 | tf_op jit(solution)/shard_map/ppermute | solution.py:78
  103.9 7.5 %collective-permute-done.8 = bf16[2,1,1,864,128]{4,3,2,1,0:T(8,128)(2,1)S(1)} collective-permute-done((bf16[2,1,1,864,128]{4,3,2,1,0:T(8,128)(2,1)S(1)}, bf16[2,1,1,864,128]{4,3,2,1,0:T(8,128)(2,1)S(1)}, u32[]{:S(2)}, u32[]{:S(2)}) %collective-permute-start.8) | collective-permute-done | bytes 442400 | tf_op jit(solution)/shard_map/ppermute | solution.py:78
  114.9 6.9 %collective-permute-done.17 = bf16[1,2,1,880,128]{4,3,2,1,0:T(8,128)(2,1)S(1)} collective-permute-done((bf16[1,2,1,880,128]{4,3,2,1,0:T(8,128)(2,1)S(1)}, bf16[1,2,1,880,128]{4,3,2,1,0:T(8,128)(2,1)S(1)}, u32[]{:S(2)}, u32[]{:S(2)}) %collective-permute-start.17) | collective-permute-done | bytes 450592 | tf_op jit(solution)/shard_map/ppermute | solution.py:78
  132.0 5.1 %unpack_g1.1 = (f32[1,768]{1,0:T(1,128)}, f32[1,768]{1,0:T(1,128)}, bf16[768,2304]{1,0:T(8,128)(2,1)}, f32[1,768]{1,0:T(1,128)}, f32[1,768]{1,0:T(1,128)}) custom-call(s32[1]{0:T(128)} %bitcast.refs_0_, bf16[8,880,128]{2,1,0:T(8,128)(2,1)} %bitcast.293, bf16[8,864,128]{2,1,0:T(8,128)(2,1)} %bitcast.295), custom_call_target="tpu_custom_call" | custom-call | bytes 7090176 | tf_op jit(solution)/shard_map/unpack_g1/pallas_call | solution.py:156
  141.1 2.8 pad_maximum_fusion.1
  143.9 2.8 unpack_wo.1
  146.7 2.6 pad_maximum_fusion.2
  149.3 7.6 %unpack_w1.1 = (bf16[768,3072]{1,0:T(8,128)(2,1)}, f32[1,3072]{1,0:T(1,128)}) custom-call(s32[1]{0:T(128)} %bitcast.refs_0_, bf16[8,880,128]{2,1,0:T(8,128)(2,1)} %bitcast.287, bf16[8,864,128]{2,1,0:T(8,128)(2,1)} %bitcast.291, bf16[8,880,128]{2,1,0:T(8,128)(2,1)} %bitcast.284, bf16[8,864,128]{2,1,0:T(8,128)(2,1)} %bitcast.288), custom_call_target="tpu_custom_call" | custom-call | bytes 9449472 | tf_op jit(solution)/shard_map/unpack_w1/pallas_call | solution.py:156
  156.9 2.7 pad_maximum_fusion.3
  159.6 5.8 %unpack_w2.1 = (bf16[3072,768]{1,0:T(8,128)(2,1)}, f32[1,768]{1,0:T(1,128)}) custom-call(s32[1]{0:T(128)} %bitcast.refs_0_, bf16[8,880,128]{2,1,0:T(8,128)(2,1)} %bitcast.285, bf16[8,864,128]{2,1,0:T(8,128)(2,1)} %bitcast.289, bf16[8,880,128]{2,1,0:T(8,128)(2,1)} %bitcast.292, bf16[8,864,128]{2,1,0:T(8,128)(2,1)} %bitcast.294), custom_call_target="tpu_custom_call" | custom-call | bytes 9440256 | tf_op jit(solution)/shard_map/unpack_w2/pallas_call | solution.py:156
  167.9 3.2 fusion.105
  172.1 1.7 copy.180
  174.4 1.7 copy.181
  178.3 2.1 multiply_reduce_fusion.1
  184.6 2.8 convolution_add_fusion.1
  191.3 11.1 %fusion.4 = (bf16[290,3072]{1,0:T(8,128)(2,1)S(1)}, f32[290,3072]{1,0:T(8,128)S(1)}) fusion(f32[3072]{0:T(1024)S(1)} %bitcast.320, bf16[290,768]{1,0:T(8,128)(2,1)S(1)} %convert_element_type.416, bf16[768,3072]{1,0:T(8,128)(2,1)} %get-tuple-element.36), kind=kOutput, calls=%fused_computation.12 | convolution fusion | flops 1427189760 | bytes 10521600 | tf_op jit(solution)/shard_map/dot_general | solution.py:330
  202.4 1.7 pad.38.refs_3_.refs_0_
  204.1 5.7 %fusion.102 = (f32[3072]{0:T(1024)}, bf16[290,3072]{1,0:T(8,128)(2,1)S(1)}) fusion(f32[290,3072]{1,0:T(8,128)S(1)} %get-tuple-element.111, bf16[290,768]{1,0:T(8,128)(2,1)S(1)} %copy-done.12, bf16[3072,768]{1,0:T(8,128)(2,1)} %get-tuple-element.38), kind=kOutput, calls=%fused_computation.252 | convolution fusion | flops 1378188288 | bytes 10521600 | tf_op jit(solution)/shard_map/dot_general | solution.py:341
  211.5 3.2 fusion.99
  217.7 1.7 multiply_reduce_fusion.2
  219.4 3.8 fusion.100
  223.4 2.0 convolution_convert_fusion.1
  226.2 1.7 pad.37.refs_6_.refs_1_
  227.9 1.7 reshape.422
  229.7 1.9 copy.188
  231.6 4.3 bitcast_convert_fusion
  235.9 2.5 fusion.106
  238.4 8.4 %fusion.45 = bf16[2,145,12,64]{1,3,2,0:T(8,128)(2,1)} fusion(bf16[2,145,12,64]{1,3,2,0:T(8,128)(2,1)} %copy.180, f32[2,12,145,145]{2,3,1,0:T(8,128)} %fusion.106, f32[2,12,145,145]{2,3,1,0:T(8,128)} %copy-done, f32[2,12,145]{2,1,0:T(8,128)S(1)} %copy-done.31), kind=kOutput, calls=%fused_computation.73 | convolution fusion | flops 69356544 | bytes 4941600 | tf_op jit(solution)/shard_map/shqk,sqhd->skhd/dot_general | solution.py:286
  246.8 8.7 %bitcast_convert_fusion.1 = (bf16[2,145,12,64]{1,3,2,0:T(8,128)(2,1)}, f32[2,12,64,145]{3,2,1,0:T(8,128)}) fusion(bf16[2,145,12,64]{1,3,2,0:T(8,128)(2,1)S(1)} %copy-done.10, f32[2,12,145,145]{2,3,1,0:T(8,128)} %fusion.106, f32[2,12,145,145]{2,3,1,0:T(8,128)} %copy-done, f32[2,12,145]{2,1,0:T(8,128)S(1)} %copy-done.31), kind=kOutput, calls=%fused_computation.67 | convolution fusion | flops 69356544 | bytes 5832480 | tf_op jit(solution)/shard_map/shqk,skhd->sqhd/dot_general | solution.py:286
  255.5 2.4 copy.220
  258.6 2.2 copy.218
  262.3 2.2 copy.219
  268.1 4.3 fusion.98
  281.6 10.1 %pack_0.1 = (bf16[8,880,128]{2,1,0:T(8,128)(2,1)}, bf16[8,864,128]{2,1,0:T(8,128)(2,1)}) custom-call(f32[1,768]{1,0:T(1,128)} %reshape.365.refs_0_, f32[1,768]{1,0:T(1,128)} %reshape.366.refs_1_, bf16[384,768]{1,0:T(8,128)(2,1)} %pad.32.refs_2_, bf16[384,2304]{1,0:T(8,128)(2,1)} %pad.33.refs_3_, f32[1,768]{1,0:T(1,128)} %reshape.367.refs_4_, ...), custom_call_target="tpu_custom_call" | custom-call | flops 1361313792 | bytes 7090176 | tf_op jit(solution)/shard_map/pack_0/pallas_call | solution.py:242
  291.7 2.6 constant_dynamic-slice_fusion.5
  296.8 16.9 %pack_2.1 = (bf16[8,880,128]{2,1,0:T(8,128)(2,1)}, bf16[8,864,128]{2,1,0:T(8,128)(2,1)}) custom-call(bf16[384,768]{1,0:T(8,128)(2,1)} %pad.36.refs_5_.refs_0_, bf16[384,3072]{1,0:T(8,128)(2,1)} %pad.37.refs_6_.refs_1_, f32[1,3072]{1,0:T(1,128)} %bitcast.315, bf16[384,3072]{1,0:T(8,128)(2,1)} %pad.38.refs_3_.refs_0_, bf16[384,768]{1,0:T(8,128)(2,1)} %pad.39.refs_4_.refs_1_), custom_call_target="tpu_custom_call" | custom-call | flops 1436811264 | bytes 7483392 | tf_op jit(solution)/shard_map/pack_2/pallas_call | solution.py:242
  313.6 12.5 %pack_1.1 = (bf16[8,880,128]{2,1,0:T(8,128)(2,1)}, bf16[8,864,128]{2,1,0:T(8,128)(2,1)}) custom-call(bf16[384,768]{1,0:T(8,128)(2,1)} %pad.34.refs_0_, bf16[384,768]{1,0:T(8,128)(2,1)} %pad.35.refs_1_, f32[1,768]{1,0:T(1,128)} %reshape.370.refs_2_, f32[1,768]{1,0:T(1,128)} %reshape.371.refs_3_, f32[1,768]{1,0:T(1,128)} %reshape.372.refs_4_, ...), custom_call_target="tpu_custom_call" | custom-call | flops 1662713856 | bytes 8659968 | tf_op jit(solution)/shard_map/pack_1/pallas_call | solution.py:242
  326.1 3.4 constant_dynamic-slice_fusion.1
  332.0 11.2 %pack_3.1 = (bf16[8,880,128]{2,1,0:T(8,128)(2,1)}, bf16[8,864,128]{2,1,0:T(8,128)(2,1)}) custom-call(bf16[384,3072]{1,0:T(8,128)(2,1)} %pad.38.refs_3_.refs_0_, bf16[384,768]{1,0:T(8,128)(2,1)} %pad.39.refs_4_.refs_1_, f32[1,768]{1,0:T(1,128)} %reshape.376.refs_2_), custom_call_target="tpu_custom_call" | custom-call | flops 1361903616 | bytes 7093248 | tf_op jit(solution)/shard_map/pack_3/pallas_call | solution.py:242
  360.7 4.4 collective-permute-done.43
  366.8 7.8 %collective-permute-done.46 = bf16[2,864,128]{2,1,0:T(8,128)(2,1)S(1)} collective-permute-done((bf16[2,864,128]{2,1,0:T(8,128)(2,1)S(1)}, bf16[2,864,128]{2,1,0:T(8,128)(2,1)S(1)}, u32[]{:S(2)}, u32[]{:S(2)}) %collective-permute-start.46) | collective-permute-done | bytes 442400 | tf_op jit(solution)/shard_map/ppermute | solution.py:78
  376.4 7.7 %collective-permute-done.49 = bf16[2,864,128]{2,1,0:T(8,128)(2,1)S(1)} collective-permute-done((bf16[2,864,128]{2,1,0:T(8,128)(2,1)S(1)}, bf16[2,864,128]{2,1,0:T(8,128)(2,1)S(1)}, u32[]{:S(2)}, u32[]{:S(2)}) %collective-permute-start.49) | collective-permute-done | bytes 442400 | tf_op jit(solution)/shard_map/ppermute | solution.py:78
  385.8 7.1 %collective-permute-done.52 = bf16[2,864,128]{2,1,0:T(8,128)(2,1)S(1)} collective-permute-done((bf16[2,864,128]{2,1,0:T(8,128)(2,1)S(1)}, bf16[2,864,128]{2,1,0:T(8,128)(2,1)S(1)}, u32[]{:S(2)}, u32[]{:S(2)}) %collective-permute-start.52) | collective-permute-done | bytes 442400 | tf_op jit(solution)/shard_map/ppermute | solution.py:78
  397.8 3.1 collective-permute-done.38
  402.7 3.0 collective-permute-done.44
  407.3 3.1 collective-permute-done.47
  412.0 3.1 collective-permute-done.50
  418.9 2.5 collective-permute-done.39
  424.8 9.0 %collective-permute-done.54 = bf16[2,864,128]{2,1,0:T(8,128)(2,1)S(1)} collective-permute-done((bf16[2,864,128]{2,1,0:T(8,128)(2,1)S(1)}, bf16[2,864,128]{2,1,0:T(8,128)(2,1)S(1)}, u32[]{:S(2)}, u32[]{:S(2)}) %collective-permute-start.54) | collective-permute-done | bytes 442400 | tf_op jit(solution)/shard_map/ppermute | solution.py:78
  433.9 1.7 collective-permute-start.55
  435.6 7.3 %collective-permute-done.40 = bf16[2,880,128]{2,1,0:T(8,128)(2,1)S(1)} collective-permute-done((bf16[2,880,128]{2,1,0:T(8,128)(2,1)S(1)}, bf16[2,880,128]{2,1,0:T(8,128)(2,1)S(1)}, u32[]{:S(2)}, u32[]{:S(2)}) %collective-permute-start.40) | collective-permute-done | bytes 450592 | tf_op jit(solution)/shard_map/ppermute | solution.py:78
  443.4 7.3 %collective-permute-done.55 = bf16[864,128]{1,0:T(8,128)(2,1)S(1)} collective-permute-done((bf16[864,128]{1,0:T(8,128)(2,1)S(1)}, bf16[864,128]{1,0:T(8,128)(2,1)S(1)}, u32[]{:S(2)}, u32[]{:S(2)}) %collective-permute-start.55) | collective-permute-done | bytes 221216 | tf_op jit(solution)/shard_map/ppermute | solution.py:78
  450.8 4.1 collective-permute-done.41
  455.0 2.4 fusion.89
  (358 shorter events, 120.3 us)
Async XLA Ops:
  0.6 21.5 %copy-start.1 = (f32[2,145,768]{2,0,1:T(2,128)S(1)}, f32[2,145,768]{2,0,1:T(2,128)}, u32[]{:S(2)}) copy-start(f32[2,145,768]{2,0,1:T(2,128)} %param.6) | copy-start | bytes 2672644
  2.0 20.0 %collective-permute-start.5 = (bf16[1,1,864,128]{3,2,1,0:T(8,128)(2,1)S(1)}, bf16[1,1,864,128]{3,2,1,0:T(8,128)(2,1)S(1)}, u32[]{:S(2)}, u32[]{:S(2)}) collective-permute-start(bf16[1,1,864,128]{3,2,1,0:T(8,128)(2,1)S(1)} %fusion.87), channel_id=1, source_target_pairs={{0,16},{1,17},{2,18},{3,19},{4,20},{5,21},{6,22},{7,23},{8,24},{9,... | collective-permute-start | bytes 663560 | tf_op jit(solution)/shard_map/ppermute | solution.py:78
  6.2 19.9 %collective-permute-start = (bf16[1,1,880,128]{3,2,1,0:T(8,128)(2,1)S(1)}, bf16[1,1,880,128]{3,2,1,0:T(8,128)(2,1)S(1)}, u32[]{:S(2)}, u32[]{:S(2)}) collective-permute-start(bf16[1,1,880,128]{3,2,1,0:T(8,128)(2,1)S(1)} %slice_bitcast_fusion), channel_id=1, source_target_pairs={{0,16},{1,17},{2,18},{3,19},{4,20},{5,21},{6,22},{7,23},{8,24},{9,... | collective-permute-start | bytes 675848 | tf_op jit(solution)/shard_map/ppermute | solution.py:78
  8.8 27.0 %copy-start.11 = (bf16[290,768]{1,0:T(8,128)(2,1)}, bf16[290,768]{1,0:T(8,128)(2,1)S(1)}, u32[]{:S(2)}) copy-start(bf16[290,768]{1,0:T(8,128)(2,1)S(1)} %convert_element_type.420) | copy-start | bytes 1336324
  9.7 130.1 %copy-start.32 = (f32[2,145]{1,0:T(2,128)}, f32[2,145]{1,0:T(2,128)S(1)}, u32[]{:S(2)}) copy-start(f32[2,145]{1,0:T(2,128)S(1)} %broadcast_multiply_fusion.5) | copy-start | bytes 3484
  22.1 13.5 %collective-permute-start.6 = (bf16[2,1,864,128]{3,2,1,0:T(8,128)(2,1)S(1)}, bf16[2,1,864,128]{3,2,1,0:T(8,128)(2,1)S(1)}, u32[]{:S(2)}, u32[]{:S(2)}) collective-permute-start(bf16[2,1,864,128]{3,2,1,0:T(8,128)(2,1)S(1)} %pad_maximum_fusion.26), channel_id=1, source_target_pairs={{0,8},{1,9},{2,10},{3,11},{4,12},{5,13},{6,14},{7,15},{8,0},{9,1},... | collective-permute-start | bytes 1327112 | tf_op jit(solution)/shard_map/ppermute | solution.py:78
  26.1 19.0 %collective-permute-start.1 = (bf16[2,1,880,128]{3,2,1,0:T(8,128)(2,1)S(1)}, bf16[2,1,880,128]{3,2,1,0:T(8,128)(2,1)S(1)}, u32[]{:S(2)}, u32[]{:S(2)}) collective-permute-start(bf16[2,1,880,128]{3,2,1,0:T(8,128)(2,1)S(1)} %pad_maximum_fusion.21), channel_id=1, source_target_pairs={{0,8},{1,9},{2,10},{3,11},{4,12},{5,13},{6,14},{7,15},{8,0},{9,1},... | collective-permute-start | bytes 1351688 | tf_op jit(solution)/shard_map/ppermute | solution.py:78
  26.9 113.0 %copy-start.35 = (f32[2,145]{1,0:T(2,128)}, f32[2,145]{1,0:T(2,128)S(1)}, u32[]{:S(2)}) copy-start(f32[2,145]{1,0:T(2,128)S(1)} %add_rsqrt_fusion.1) | copy-start | bytes 3484
  35.7 23.7 %collective-permute-start.25 = (bf16[1,1,1,864,128]{4,3,2,1,0:T(8,128)(2,1)S(1)}, bf16[1,1,1,864,128]{4,3,2,1,0:T(8,128)(2,1)S(1)}, u32[]{:S(2)}, u32[]{:S(2)}) collective-permute-start(bf16[1,1,1,864,128]{4,3,2,1,0:T(8,128)(2,1)S(1)} %get-tuple-element.104), channel_id=1, source_target_pairs={{0,4},{1,5},{2,6},{3,7},{4,0},{5,1},{6,2},{7,3},{8,12},{9,13},{10,... | collective-permute-start | bytes 663560 | tf_op jit(solution)/shard_map/ppermute | solution.py:78
  37.4 23.8 %collective-permute-start.19 = (bf16[1,1,1,864,128]{4,3,2,1,0:T(8,128)(2,1)S(1)}, bf16[1,1,1,864,128]{4,3,2,1,0:T(8,128)(2,1)S(1)}, u32[]{:S(2)}, u32[]{:S(2)}) collective-permute-start(bf16[1,1,1,864,128]{4,3,2,1,0:T(8,128)(2,1)S(1)} %get-tuple-element.105), channel_id=1, source_target_pairs={{0,4},{1,5},{2,6},{3,7},{4,0},{5,1},{6,2},{7,3},{8,12},{9,13},{10,... | collective-permute-start | bytes 663560 | tf_op jit(solution)/shard_map/ppermute | solution.py:78
  37.8 21.0 %collective-permute-start.13 = (bf16[1,1,1,864,128]{4,3,2,1,0:T(8,128)(2,1)S(1)}, bf16[1,1,1,864,128]{4,3,2,1,0:T(8,128)(2,1)S(1)}, u32[]{:S(2)}, u32[]{:S(2)}) collective-permute-start(bf16[1,1,1,864,128]{4,3,2,1,0:T(8,128)(2,1)S(1)} %get-tuple-element.106), channel_id=1, source_target_pairs={{0,4},{1,5},{2,6},{3,7},{4,0},{5,1},{6,2},{7,3},{8,12},{9,13},{10,... | collective-permute-start | bytes 663560 | tf_op jit(solution)/shard_map/ppermute | solution.py:78
  39.4 17.9 %collective-permute-start.7 = (bf16[1,1,1,864,128]{4,3,2,1,0:T(8,128)(2,1)S(1)}, bf16[1,1,1,864,128]{4,3,2,1,0:T(8,128)(2,1)S(1)}, u32[]{:S(2)}, u32[]{:S(2)}) collective-permute-start(bf16[1,1,1,864,128]{4,3,2,1,0:T(8,128)(2,1)S(1)} %get-tuple-element.107), channel_id=1, source_target_pairs={{0,4},{1,5},{2,6},{3,7},{4,0},{5,1},{6,2},{7,3},{8,12},{9,13},{10,... | collective-permute-start | bytes 663560 | tf_op jit(solution)/shard_map/ppermute | solution.py:78
  45.3 31.6 %collective-permute-start.22 = (bf16[1,1,1,880,128]{4,3,2,1,0:T(8,128)(2,1)S(1)}, bf16[1,1,1,880,128]{4,3,2,1,0:T(8,128)(2,1)S(1)}, u32[]{:S(2)}, u32[]{:S(2)}) collective-permute-start(bf16[1,1,1,880,128]{4,3,2,1,0:T(8,128)(2,1)S(1)} %get-tuple-element.98), channel_id=1, source_target_pairs={{0,2},{1,3},{2,0},{3,1},{4,6},{5,7},{6,4},{7,5},{8,10},{9,11},{10,... | collective-permute-start | bytes 675848 | tf_op jit(solution)/shard_map/ppermute | solution.py:78
  57.3 20.2 %collective-permute-start.16 = (bf16[1,1,1,880,128]{4,3,2,1,0:T(8,128)(2,1)S(1)}, bf16[1,1,1,880,128]{4,3,2,1,0:T(8,128)(2,1)S(1)}, u32[]{:S(2)}, u32[]{:S(2)}) collective-permute-start(bf16[1,1,1,880,128]{4,3,2,1,0:T(8,128)(2,1)S(1)} %get-tuple-element.99), channel_id=1, source_target_pairs={{0,2},{1,3},{2,0},{3,1},{4,6},{5,7},{6,4},{7,5},{8,10},{9,11},{10,... | collective-permute-start | bytes 675848 | tf_op jit(solution)/shard_map/ppermute | solution.py:78
  58.9 20.3 %collective-permute-start.10 = (bf16[1,1,1,880,128]{4,3,2,1,0:T(8,128)(2,1)S(1)}, bf16[1,1,1,880,128]{4,3,2,1,0:T(8,128)(2,1)S(1)}, u32[]{:S(2)}, u32[]{:S(2)}) collective-permute-start(bf16[1,1,1,880,128]{4,3,2,1,0:T(8,128)(2,1)S(1)} %get-tuple-element.100), channel_id=1, source_target_pairs={{0,2},{1,3},{2,0},{3,1},{4,6},{5,7},{6,4},{7,5},{8,10},{9,11},{10,... | collective-permute-start | bytes 675848 | tf_op jit(solution)/shard_map/ppermute | solution.py:78
  59.5 15.8 %collective-permute-start.2 = (bf16[1,1,1,880,128]{4,3,2,1,0:T(8,128)(2,1)S(1)}, bf16[1,1,1,880,128]{4,3,2,1,0:T(8,128)(2,1)S(1)}, u32[]{:S(2)}, u32[]{:S(2)}) collective-permute-start(bf16[1,1,1,880,128]{4,3,2,1,0:T(8,128)(2,1)S(1)} %get-tuple-element.101), channel_id=1, source_target_pairs={{0,2},{1,3},{2,0},{3,1},{4,6},{5,7},{6,4},{7,5},{8,10},{9,11},{10,... | collective-permute-start | bytes 675848 | tf_op jit(solution)/shard_map/ppermute | solution.py:78
  61.1 23.7 %collective-permute-start.26 = (bf16[2,1,1,864,128]{4,3,2,1,0:T(8,128)(2,1)S(1)}, bf16[2,1,1,864,128]{4,3,2,1,0:T(8,128)(2,1)S(1)}, u32[]{:S(2)}, u32[]{:S(2)}) collective-permute-start(bf16[2,1,1,864,128]{4,3,2,1,0:T(8,128)(2,1)S(1)} %pad_maximum_fusion.30), channel_id=1, source_target_pairs={{0,2},{1,3},{2,0},{3,1},{4,6},{5,7},{6,4},{7,5},{8,10},{9,11},{10,... | collective-permute-start | bytes 1327112 | tf_op jit(solution)/shard_map/ppermute | solution.py:78
  75.3 19.0 %collective-permute-start.20 = (bf16[2,1,1,864,128]{4,3,2,1,0:T(8,128)(2,1)S(1)}, bf16[2,1,1,864,128]{4,3,2,1,0:T(8,128)(2,1)S(1)}, u32[]{:S(2)}, u32[]{:S(2)}) collective-permute-start(bf16[2,1,1,864,128]{4,3,2,1,0:T(8,128)(2,1)S(1)} %pad_maximum_fusion.29), channel_id=1, source_target_pairs={{0,2},{1,3},{2,0},{3,1},{4,6},{5,7},{6,4},{7,5},{8,10},{9,11},{10,... | collective-permute-start | bytes 1327112 | tf_op jit(solution)/shard_map/ppermute | solution.py:78
  76.9 26.8 %collective-permute-start.14 = (bf16[2,1,1,864,128]{4,3,2,1,0:T(8,128)(2,1)S(1)}, bf16[2,1,1,864,128]{4,3,2,1,0:T(8,128)(2,1)S(1)}, u32[]{:S(2)}, u32[]{:S(2)}) collective-permute-start(bf16[2,1,1,864,128]{4,3,2,1,0:T(8,128)(2,1)S(1)} %pad_maximum_fusion.28), channel_id=1, source_target_pairs={{0,2},{1,3},{2,0},{3,1},{4,6},{5,7},{6,4},{7,5},{8,10},{9,11},{10,... | collective-permute-start | bytes 1327112 | tf_op jit(solution)/shard_map/ppermute | solution.py:78
  77.5 33.8 %collective-permute-start.8 = (bf16[2,1,1,864,128]{4,3,2,1,0:T(8,128)(2,1)S(1)}, bf16[2,1,1,864,128]{4,3,2,1,0:T(8,128)(2,1)S(1)}, u32[]{:S(2)}, u32[]{:S(2)}) collective-permute-start(bf16[2,1,1,864,128]{4,3,2,1,0:T(8,128)(2,1)S(1)} %pad_maximum_fusion.27), channel_id=1, source_target_pairs={{0,2},{1,3},{2,0},{3,1},{4,6},{5,7},{6,4},{7,5},{8,10},{9,11},{10,... | collective-permute-start | bytes 1327112 | tf_op jit(solution)/shard_map/ppermute | solution.py:78
  79.1 33.8 %collective-permute-start.23 = (bf16[1,2,1,880,128]{4,3,2,1,0:T(8,128)(2,1)S(1)}, bf16[1,2,1,880,128]{4,3,2,1,0:T(8,128)(2,1)S(1)}, u32[]{:S(2)}, u32[]{:S(2)}) collective-permute-start(bf16[1,2,1,880,128]{4,3,2,1,0:T(8,128)(2,1)S(1)} %pad_maximum_fusion.25), channel_id=1, source_target_pairs={{0,4},{1,5},{2,6},{3,7},{4,0},{5,1},{6,2},{7,3},{8,12},{9,13},{10,... | collective-permute-start | bytes 1351688 | tf_op jit(solution)/shard_map/ppermute | solution.py:78
  84.8 28.2 %collective-permute-start.11 = (bf16[1,2,1,880,128]{4,3,2,1,0:T(8,128)(2,1)S(1)}, bf16[1,2,1,880,128]{4,3,2,1,0:T(8,128)(2,1)S(1)}, u32[]{:S(2)}, u32[]{:S(2)}) collective-permute-start(bf16[1,2,1,880,128]{4,3,2,1,0:T(8,128)(2,1)S(1)} %pad_maximum_fusion.23), channel_id=1, source_target_pairs={{0,4},{1,5},{2,6},{3,7},{4,0},{5,1},{6,2},{7,3},{8,12},{9,13},{10,... | collective-permute-start | bytes 1351688 | tf_op jit(solution)/shard_map/ppermute | solution.py:78
  94.3 19.4 %collective-permute-start.3 = (bf16[1,2,1,880,128]{4,3,2,1,0:T(8,128)(2,1)S(1)}, bf16[1,2,1,880,128]{4,3,2,1,0:T(8,128)(2,1)S(1)}, u32[]{:S(2)}, u32[]{:S(2)}) collective-permute-start(bf16[1,2,1,880,128]{4,3,2,1,0:T(8,128)(2,1)S(1)} %pad_maximum_fusion.22), channel_id=1, source_target_pairs={{0,4},{1,5},{2,6},{3,7},{4,0},{5,1},{6,2},{7,3},{8,12},{9,13},{10,... | collective-permute-start | bytes 1351688 | tf_op jit(solution)/shard_map/ppermute | solution.py:78
  103.8 20.1 %collective-permute-start.27 = (bf16[2,2,1,864,128]{4,3,2,1,0:T(8,128)(2,1)S(1)}, bf16[2,2,1,864,128]{4,3,2,1,0:T(8,128)(2,1)S(1)}, u32[]{:S(2)}, u32[]{:S(2)}) collective-permute-start(bf16[2,2,1,864,128]{4,3,2,1,0:T(8,128)(2,1)S(1)} %pad_maximum_fusion.19), channel_id=1, source_target_pairs={{0,1},{1,0},{2,3},{3,2},{4,5},{5,4},{6,7},{7,6},{8,9},{9,8},{10,11... | collective-permute-start | bytes 2654216 | tf_op jit(solution)/shard_map/ppermute | solution.py:78
  111.3 10.5 %collective-permute-start.17 = (bf16[1,2,1,880,128]{4,3,2,1,0:T(8,128)(2,1)S(1)}, bf16[1,2,1,880,128]{4,3,2,1,0:T(8,128)(2,1)S(1)}, u32[]{:S(2)}, u32[]{:S(2)}) collective-permute-start(bf16[1,2,1,880,128]{4,3,2,1,0:T(8,128)(2,1)S(1)} %pad_maximum_fusion.24), channel_id=1, source_target_pairs={{0,4},{1,5},{2,6},{3,7},{4,0},{5,1},{6,2},{7,3},{8,12},{9,13},{10,... | collective-permute-start | bytes 1351688 | tf_op jit(solution)/shard_map/ppermute | solution.py:78
  112.9 12.9 %collective-permute-start.21 = (bf16[2,2,1,864,128]{4,3,2,1,0:T(8,128)(2,1)S(1)}, bf16[2,2,1,864,128]{4,3,2,1,0:T(8,128)(2,1)S(1)}, u32[]{:S(2)}, u32[]{:S(2)}) collective-permute-start(bf16[2,2,1,864,128]{4,3,2,1,0:T(8,128)(2,1)S(1)} %pad_maximum_fusion.18), channel_id=1, source_target_pairs={{0,1},{1,0},{2,3},{3,2},{4,5},{5,4},{6,7},{7,6},{8,9},{9,8},{10,11... | collective-permute-start | bytes 2654216 | tf_op jit(solution)/shard_map/ppermute | solution.py:78
  113.0 10.9 %copy-start.18 = (bf16[1,2,1,880,128]{4,3,2,1,0:T(8,128)(2,1)}, bf16[1,2,1,880,128]{4,3,2,1,0:T(8,128)(2,1)S(1)}, u32[]{:S(2)}) copy-start(bf16[1,2,1,880,128]{4,3,2,1,0:T(8,128)(2,1)S(1)} %collective-permute-done.11) | copy-start | bytes 1351684
  113.0 14.2 %collective-permute-start.15 = (bf16[2,2,1,864,128]{4,3,2,1,0:T(8,128)(2,1)S(1)}, bf16[2,2,1,864,128]{4,3,2,1,0:T(8,128)(2,1)S(1)}, u32[]{:S(2)}, u32[]{:S(2)}) collective-permute-start(bf16[2,2,1,864,128]{4,3,2,1,0:T(8,128)(2,1)S(1)} %pad_maximum_fusion.17), channel_id=1, source_target_pairs={{0,1},{1,0},{2,3},{3,2},{4,5},{5,4},{6,7},{7,6},{8,9},{9,8},{10,11... | collective-permute-start | bytes 2654216 | tf_op jit(solution)/shard_map/ppermute | solution.py:78
  113.7 15.5 %collective-permute-start.9 = (bf16[2,2,1,864,128]{4,3,2,1,0:T(8,128)(2,1)S(1)}, bf16[2,2,1,864,128]{4,3,2,1,0:T(8,128)(2,1)S(1)}, u32[]{:S(2)}, u32[]{:S(2)}) collective-permute-start(bf16[2,2,1,864,128]{4,3,2,1,0:T(8,128)(2,1)S(1)} %pad_maximum_fusion.16), channel_id=1, source_target_pairs={{0,1},{1,0},{2,3},{3,2},{4,5},{5,4},{6,7},{7,6},{8,9},{9,8},{10,11... | collective-permute-start | bytes 2654216 | tf_op jit(solution)/shard_map/ppermute | solution.py:78
  121.8 8.8 %collective-permute-start.4 = (bf16[2,2,1,880,128]{4,3,2,1,0:T(8,128)(2,1)S(1)}, bf16[2,2,1,880,128]{4,3,2,1,0:T(8,128)(2,1)S(1)}, u32[]{:S(2)}, u32[]{:S(2)}) collective-permute-start(bf16[2,2,1,880,128]{4,3,2,1,0:T(8,128)(2,1)S(1)} %pad_maximum_fusion.9), channel_id=1, source_target_pairs={{0,1},{1,0},{2,3},{3,2},{4,5},{5,4},{6,7},{7,6},{8,9},{9,8},{10,11... | collective-permute-start | bytes 2703368 | tf_op jit(solution)/shard_map/ppermute | solution.py:78
  123.9 17.2 %collective-permute-start.12 = (bf16[2,2,1,880,128]{4,3,2,1,0:T(8,128)(2,1)}, bf16[2,2,1,880,128]{4,3,2,1,0:T(8,128)(2,1)}, u32[]{:S(2)}, u32[]{:S(2)}) collective-permute-start(bf16[2,2,1,880,128]{4,3,2,1,0:T(8,128)(2,1)} %pad_maximum_fusion.10), channel_id=1, source_target_pairs={{0,1},{1,0},{2,3},{3,2},{4,5},{5,4},{6,7},{7,6},{8,9},{9,8},{10,11... | collective-permute-start | bytes 2703368 | tf_op jit(solution)/shard_map/ppermute | solution.py:78
  125.8 31.1 %collective-permute-start.24 = (bf16[2,2,1,880,128]{4,3,2,1,0:T(8,128)(2,1)}, bf16[2,2,1,880,128]{4,3,2,1,0:T(8,128)(2,1)}, u32[]{:S(2)}, u32[]{:S(2)}) collective-permute-start(bf16[2,2,1,880,128]{4,3,2,1,0:T(8,128)(2,1)} %pad_maximum_fusion.12), channel_id=1, source_target_pairs={{0,1},{1,0},{2,3},{3,2},{4,5},{5,4},{6,7},{7,6},{8,9},{9,8},{10,11... | collective-permute-start | bytes 2703368 | tf_op jit(solution)/shard_map/ppermute | solution.py:78
  127.3 19.4 %collective-permute-start.18 = (bf16[2,2,1,880,128]{4,3,2,1,0:T(8,128)(2,1)}, bf16[2,2,1,880,128]{4,3,2,1,0:T(8,128)(2,1)}, u32[]{:S(2)}, u32[]{:S(2)}) collective-permute-start(bf16[2,2,1,880,128]{4,3,2,1,0:T(8,128)(2,1)} %pad_maximum_fusion.11), channel_id=1, source_target_pairs={{0,1},{1,0},{2,3},{3,2},{4,5},{5,4},{6,7},{7,6},{8,9},{9,8},{10,11... | collective-permute-start | bytes 2703368 | tf_op jit(solution)/shard_map/ppermute | solution.py:78
  295.3 51.0 %collective-permute-start.42 = (bf16[2,2,864,128]{3,2,0,1:T(8,128)(2,1)}, bf16[2,2,864,128]{3,2,0,1:T(8,128)(2,1)}, u32[]{:S(2)}, u32[]{:S(2)}) collective-permute-start(bf16[2,2,864,128]{3,2,0,1:T(8,128)(2,1)} %bitcast.282), channel_id=1, source_target_pairs={{0,1},{1,0},{2,3},{3,2},{4,5},{5,4},{6,7},{7,6},{8,9},{9,8},{10,11... | collective-permute-start | bytes 2654216 | tf_op jit(solution)/shard_map/ppermute | solution.py:78
  296.3 57.7 %collective-permute-start.28 = (bf16[2,2,880,128]{3,2,1,0:T(8,128)(2,1)}, bf16[2,2,880,128]{3,2,1,0:T(8,128)(2,1)}, u32[]{:S(2)}, u32[]{:S(2)}) collective-permute-start(bf16[2,2,880,128]{3,2,1,0:T(8,128)(2,1)} %dynamic-slice_bitcast_fusion.3), channel_id=1, source_target_pairs={{0,1},{1,0},{2,3},{3,2},{4,5},{5,4},{6,7},{7,6},{8,9},{9,8},{10,11... | collective-permute-start | bytes 2703368 | tf_op jit(solution)/shard_map/ppermute | solution.py:78
  331.5 16.7 %collective-permute-start.45 = (bf16[2,2,864,128]{3,2,0,1:T(8,128)(2,1)}, bf16[2,2,864,128]{3,2,0,1:T(8,128)(2,1)}, u32[]{:S(2)}, u32[]{:S(2)}) collective-permute-start(bf16[2,2,864,128]{3,2,0,1:T(8,128)(2,1)} %bitcast.281), channel_id=1, source_target_pairs={{0,1},{1,0},{2,3},{3,2},{4,5},{5,4},{6,7},{7,6},{8,9},{9,8},{10,11... | collective-permute-start | bytes 2654216 | tf_op jit(solution)/shard_map/ppermute | solution.py:78
  331.5 18.6 %collective-permute-start.48 = (bf16[2,2,864,128]{3,2,0,1:T(8,128)(2,1)}, bf16[2,2,864,128]{3,2,0,1:T(8,128)(2,1)}, u32[]{:S(2)}, u32[]{:S(2)}) collective-permute-start(bf16[2,2,864,128]{3,2,0,1:T(8,128)(2,1)} %bitcast.280), channel_id=1, source_target_pairs={{0,1},{1,0},{2,3},{3,2},{4,5},{5,4},{6,7},{7,6},{8,9},{9,8},{10,11... | collective-permute-start | bytes 2654216 | tf_op jit(solution)/shard_map/ppermute | solution.py:78
  344.6 7.4 %collective-permute-start.51 = (bf16[2,2,864,128]{3,2,1,0:T(8,128)(2,1)S(1)}, bf16[2,2,864,128]{3,2,1,0:T(8,128)(2,1)S(1)}, u32[]{:S(2)}, u32[]{:S(2)}) collective-permute-start(bf16[2,2,864,128]{3,2,1,0:T(8,128)(2,1)S(1)} %dynamic-slice_bitcast_fusion.4), channel_id=1, source_target_pairs={{0,1},{1,0},{2,3},{3,2},{4,5},{5,4},{6,7},{7,6},{8,9},{9,8},{10,11... | collective-permute-start | bytes 2654216 | tf_op jit(solution)/shard_map/ppermute | solution.py:78
  346.3 9.7 %collective-permute-start.31 = (bf16[2,2,880,128]{3,2,1,0:T(8,128)(2,1)S(1)}, bf16[2,2,880,128]{3,2,1,0:T(8,128)(2,1)S(1)}, u32[]{:S(2)}, u32[]{:S(2)}) collective-permute-start(bf16[2,2,880,128]{3,2,1,0:T(8,128)(2,1)S(1)} %dynamic-slice_bitcast_fusion.2), channel_id=1, source_target_pairs={{0,1},{1,0},{2,3},{3,2},{4,5},{5,4},{6,7},{7,6},{8,9},{9,8},{10,11... | collective-permute-start | bytes 2703368 | tf_op jit(solution)/shard_map/ppermute | solution.py:78
  348.2 9.7 %collective-permute-start.34 = (bf16[2,2,880,128]{3,2,1,0:T(8,128)(2,1)S(1)}, bf16[2,2,880,128]{3,2,1,0:T(8,128)(2,1)S(1)}, u32[]{:S(2)}, u32[]{:S(2)}) collective-permute-start(bf16[2,2,880,128]{3,2,1,0:T(8,128)(2,1)S(1)} %dynamic-slice_bitcast_fusion.1), channel_id=1, source_target_pairs={{0,1},{1,0},{2,3},{3,2},{4,5},{5,4},{6,7},{7,6},{8,9},{9,8},{10,11... | collective-permute-start | bytes 2703368 | tf_op jit(solution)/shard_map/ppermute | solution.py:78
  350.1 8.5 %collective-permute-start.37 = (bf16[2,2,880,128]{3,2,1,0:T(8,128)(2,1)S(1)}, bf16[2,2,880,128]{3,2,1,0:T(8,128)(2,1)S(1)}, u32[]{:S(2)}, u32[]{:S(2)}) collective-permute-start(bf16[2,2,880,128]{3,2,1,0:T(8,128)(2,1)S(1)} %dynamic-slice_bitcast_fusion), channel_id=1, source_target_pairs={{0,1},{1,0},{2,3},{3,2},{4,5},{5,4},{6,7},{7,6},{8,9},{9,8},{10,11... | collective-permute-start | bytes 2703368 | tf_op jit(solution)/shard_map/ppermute | solution.py:78
  352.0 13.1 %collective-permute-start.43 = (bf16[2,864,128]{2,1,0:T(8,128)(2,1)S(1)}, bf16[2,864,128]{2,1,0:T(8,128)(2,1)S(1)}, u32[]{:S(2)}, u32[]{:S(2)}) collective-permute-start(bf16[2,864,128]{2,1,0:T(8,128)(2,1)S(1)} %dynamic-slice_bitcast_fusion.14), channel_id=1, source_target_pairs={{0,2},{1,3},{2,0},{3,1},{4,6},{5,7},{6,4},{7,5},{8,10},{9,11},{10,... | collective-permute-start | bytes 1327112 | tf_op jit(solution)/shard_map/ppermute | solution.py:78
  354.0 20.6 %collective-permute-start.46 = (bf16[2,864,128]{2,1,0:T(8,128)(2,1)S(1)}, bf16[2,864,128]{2,1,0:T(8,128)(2,1)S(1)}, u32[]{:S(2)}, u32[]{:S(2)}) collective-permute-start(bf16[2,864,128]{2,1,0:T(8,128)(2,1)S(1)} %dynamic-slice_bitcast_fusion.13), channel_id=1, source_target_pairs={{0,2},{1,3},{2,0},{3,1},{4,6},{5,7},{6,4},{7,5},{8,10},{9,11},{10,... | collective-permute-start | bytes 1327112 | tf_op jit(solution)/shard_map/ppermute | solution.py:78
  356.0 28.1 %collective-permute-start.49 = (bf16[2,864,128]{2,1,0:T(8,128)(2,1)S(1)}, bf16[2,864,128]{2,1,0:T(8,128)(2,1)S(1)}, u32[]{:S(2)}, u32[]{:S(2)}) collective-permute-start(bf16[2,864,128]{2,1,0:T(8,128)(2,1)S(1)} %dynamic-slice_bitcast_fusion.12), channel_id=1, source_target_pairs={{0,2},{1,3},{2,0},{3,1},{4,6},{5,7},{6,4},{7,5},{8,10},{9,11},{10,... | collective-permute-start | bytes 1327112 | tf_op jit(solution)/shard_map/ppermute | solution.py:78
  357.9 35.0 %collective-permute-start.52 = (bf16[2,864,128]{2,1,0:T(8,128)(2,1)S(1)}, bf16[2,864,128]{2,1,0:T(8,128)(2,1)S(1)}, u32[]{:S(2)}, u32[]{:S(2)}) collective-permute-start(bf16[2,864,128]{2,1,0:T(8,128)(2,1)S(1)} %dynamic-slice_bitcast_fusion.11), channel_id=1, source_target_pairs={{0,2},{1,3},{2,0},{3,1},{4,6},{5,7},{6,4},{7,5},{8,10},{9,11},{10,... | collective-permute-start | bytes 1327112 | tf_op jit(solution)/shard_map/ppermute | solution.py:78
  358.7 36.0 %collective-permute-start.29 = (bf16[2,880,128]{2,1,0:T(8,128)(2,1)S(1)}, bf16[2,880,128]{2,1,0:T(8,128)(2,1)S(1)}, u32[]{:S(2)}, u32[]{:S(2)}) collective-permute-start(bf16[2,880,128]{2,1,0:T(8,128)(2,1)S(1)} %dynamic-slice_bitcast_fusion.9), channel_id=1, source_target_pairs={{0,4},{1,5},{2,6},{3,7},{4,0},{5,1},{6,2},{7,3},{8,12},{9,13},{10,... | collective-permute-start | bytes 1351688 | tf_op jit(solution)/shard_map/ppermute | solution.py:78
  365.1 30.2 %collective-permute-start.32 = (bf16[2,880,128]{2,1,0:T(8,128)(2,1)S(1)}, bf16[2,880,128]{2,1,0:T(8,128)(2,1)S(1)}, u32[]{:S(2)}, u32[]{:S(2)}) collective-permute-start(bf16[2,880,128]{2,1,0:T(8,128)(2,1)S(1)} %dynamic-slice_bitcast_fusion.8), channel_id=1, source_target_pairs={{0,4},{1,5},{2,6},{3,7},{4,0},{5,1},{6,2},{7,3},{8,12},{9,13},{10,... | collective-permute-start | bytes 1351688 | tf_op jit(solution)/shard_map/ppermute | solution.py:78
  374.6 22.5 %collective-permute-start.35 = (bf16[2,880,128]{2,1,0:T(8,128)(2,1)S(1)}, bf16[2,880,128]{2,1,0:T(8,128)(2,1)S(1)}, u32[]{:S(2)}, u32[]{:S(2)}) collective-permute-start(bf16[2,880,128]{2,1,0:T(8,128)(2,1)S(1)} %dynamic-slice_bitcast_fusion.7), channel_id=1, source_target_pairs={{0,4},{1,5},{2,6},{3,7},{4,0},{5,1},{6,2},{7,3},{8,12},{9,13},{10,... | collective-permute-start | bytes 1351688 | tf_op jit(solution)/shard_map/ppermute | solution.py:78
  384.1 16.8 %collective-permute-start.38 = (bf16[2,880,128]{2,1,0:T(8,128)(2,1)S(1)}, bf16[2,880,128]{2,1,0:T(8,128)(2,1)S(1)}, u32[]{:S(2)}, u32[]{:S(2)}) collective-permute-start(bf16[2,880,128]{2,1,0:T(8,128)(2,1)S(1)} %dynamic-slice_bitcast_fusion.6), channel_id=1, source_target_pairs={{0,4},{1,5},{2,6},{3,7},{4,0},{5,1},{6,2},{7,3},{8,12},{9,13},{10,... | collective-permute-start | bytes 1351688 | tf_op jit(solution)/shard_map/ppermute | solution.py:78
  392.9 12.8 %collective-permute-start.44 = (bf16[864,128]{1,0:T(8,128)(2,1)S(1)}, bf16[864,128]{1,0:T(8,128)(2,1)S(1)}, u32[]{:S(2)}, u32[]{:S(2)}) collective-permute-start(bf16[864,128]{1,0:T(8,128)(2,1)S(1)} %dynamic-slice_bitcast_fusion.28), channel_id=1, source_target_pairs={{0,4},{1,5},{2,6},{3,7},{4,0},{5,1},{6,2},{7,3},{8,12},{9,13},{10,... | collective-permute-start | bytes 663560 | tf_op jit(solution)/shard_map/ppermute | solution.py:78
  394.6 15.8 %collective-permute-start.47 = (bf16[864,128]{1,0:T(8,128)(2,1)S(1)}, bf16[864,128]{1,0:T(8,128)(2,1)S(1)}, u32[]{:S(2)}, u32[]{:S(2)}) collective-permute-start(bf16[864,128]{1,0:T(8,128)(2,1)S(1)} %dynamic-slice_bitcast_fusion.27), channel_id=1, source_target_pairs={{0,4},{1,5},{2,6},{3,7},{4,0},{5,1},{6,2},{7,3},{8,12},{9,13},{10,... | collective-permute-start | bytes 663560 | tf_op jit(solution)/shard_map/ppermute | solution.py:78
  395.3 19.8 %collective-permute-start.50 = (bf16[864,128]{1,0:T(8,128)(2,1)S(1)}, bf16[864,128]{1,0:T(8,128)(2,1)S(1)}, u32[]{:S(2)}, u32[]{:S(2)}) collective-permute-start(bf16[864,128]{1,0:T(8,128)(2,1)S(1)} %dynamic-slice_bitcast_fusion.26), channel_id=1, source_target_pairs={{0,4},{1,5},{2,6},{3,7},{4,0},{5,1},{6,2},{7,3},{8,12},{9,13},{10,... | collective-permute-start | bytes 663560 | tf_op jit(solution)/shard_map/ppermute | solution.py:78
  397.1 20.9 %collective-permute-start.53 = (bf16[864,128]{1,0:T(8,128)(2,1)S(1)}, bf16[864,128]{1,0:T(8,128)(2,1)S(1)}, u32[]{:S(2)}, u32[]{:S(2)}) collective-permute-start(bf16[864,128]{1,0:T(8,128)(2,1)S(1)} %dynamic-slice_bitcast_fusion.25), channel_id=1, source_target_pairs={{0,4},{1,5},{2,6},{3,7},{4,0},{5,1},{6,2},{7,3},{8,12},{9,13},{10,... | collective-permute-start | bytes 663560 | tf_op jit(solution)/shard_map/ppermute | solution.py:78
  400.9 17.5 %collective-permute-start.30 = (bf16[880,128]{1,0:T(8,128)(2,1)S(1)}, bf16[880,128]{1,0:T(8,128)(2,1)S(1)}, u32[]{:S(2)}, u32[]{:S(2)}) collective-permute-start(bf16[880,128]{1,0:T(8,128)(2,1)S(1)} %dynamic-slice_bitcast_fusion.19), channel_id=1, source_target_pairs={{0,2},{1,3},{2,0},{3,1},{4,6},{5,7},{6,4},{7,5},{8,10},{9,11},{10,... | collective-permute-start | bytes 675848 | tf_op jit(solution)/shard_map/ppermute | solution.py:78
  405.7 12.8 %collective-permute-start.33 = (bf16[880,128]{1,0:T(8,128)(2,1)S(1)}, bf16[880,128]{1,0:T(8,128)(2,1)S(1)}, u32[]{:S(2)}, u32[]{:S(2)}) collective-permute-start(bf16[880,128]{1,0:T(8,128)(2,1)S(1)} %dynamic-slice_bitcast_fusion.18), channel_id=1, source_target_pairs={{0,2},{1,3},{2,0},{3,1},{4,6},{5,7},{6,4},{7,5},{8,10},{9,11},{10,... | collective-permute-start | bytes 675848 | tf_op jit(solution)/shard_map/ppermute | solution.py:78
  410.4 8.4 %collective-permute-start.36 = (bf16[880,128]{1,0:T(8,128)(2,1)S(1)}, bf16[880,128]{1,0:T(8,128)(2,1)S(1)}, u32[]{:S(2)}, u32[]{:S(2)}) collective-permute-start(bf16[880,128]{1,0:T(8,128)(2,1)S(1)} %dynamic-slice_bitcast_fusion.17), channel_id=1, source_target_pairs={{0,2},{1,3},{2,0},{3,1},{4,6},{5,7},{6,4},{7,5},{8,10},{9,11},{10,... | collective-permute-start | bytes 675848 | tf_op jit(solution)/shard_map/ppermute | solution.py:78
  415.1 6.2 %collective-permute-start.39 = (bf16[880,128]{1,0:T(8,128)(2,1)S(1)}, bf16[880,128]{1,0:T(8,128)(2,1)S(1)}, u32[]{:S(2)}, u32[]{:S(2)}) collective-permute-start(bf16[880,128]{1,0:T(8,128)(2,1)S(1)} %dynamic-slice_bitcast_fusion.16), channel_id=1, source_target_pairs={{0,2},{1,3},{2,0},{3,1},{4,6},{5,7},{6,4},{7,5},{8,10},{9,11},{10,... | collective-permute-start | bytes 675848 | tf_op jit(solution)/shard_map/ppermute | solution.py:78
  418.3 15.5 %collective-permute-start.54 = (bf16[2,864,128]{2,1,0:T(8,128)(2,1)S(1)}, bf16[2,864,128]{2,1,0:T(8,128)(2,1)S(1)}, u32[]{:S(2)}, u32[]{:S(2)}) collective-permute-start(bf16[2,864,128]{2,1,0:T(8,128)(2,1)S(1)} %dynamic-slice_bitcast_fusion.10), channel_id=1, source_target_pairs={{0,8},{1,9},{2,10},{3,11},{4,12},{5,13},{6,14},{7,15},{8,0},{9,1},... | collective-permute-start | bytes 1327112 | tf_op jit(solution)/shard_map/ppermute | solution.py:78
  421.6 21.3 %collective-permute-start.40 = (bf16[2,880,128]{2,1,0:T(8,128)(2,1)S(1)}, bf16[2,880,128]{2,1,0:T(8,128)(2,1)S(1)}, u32[]{:S(2)}, u32[]{:S(2)}) collective-permute-start(bf16[2,880,128]{2,1,0:T(8,128)(2,1)S(1)} %dynamic-slice_bitcast_fusion.5), channel_id=1, source_target_pairs={{0,8},{1,9},{2,10},{3,11},{4,12},{5,13},{6,14},{7,15},{8,0},{9,1},... | collective-permute-start | bytes 1351688 | tf_op jit(solution)/shard_map/ppermute | solution.py:78
  423.4 31.5 %copy-start.6 = (f32[221568]{0:T(1024)S(1)}, f32[221568]{0:T(1024)}, u32[]{:S(2)}) copy-start(f32[221568]{0:T(1024)} %param.9) | copy-start | bytes 2658820
  423.4 31.6 %copy-start.28 = (f32[221568]{0:T(1024)S(1)}, f32[221568]{0:T(1024)}, u32[]{:S(2)}) copy-start(f32[221568]{0:T(1024)} %param.11) | copy-start | bytes 2658820
  423.4 31.6 %copy-start.29 = (f32[221568]{0:T(1024)S(1)}, f32[221568]{0:T(1024)}, u32[]{:S(2)}) copy-start(f32[221568]{0:T(1024)} %param.10) | copy-start | bytes 2658820
  433.9 16.8 %collective-permute-start.55 = (bf16[864,128]{1,0:T(8,128)(2,1)S(1)}, bf16[864,128]{1,0:T(8,128)(2,1)S(1)}, u32[]{:S(2)}, u32[]{:S(2)}) collective-permute-start(bf16[864,128]{1,0:T(8,128)(2,1)S(1)} %dynamic-slice_bitcast_fusion.24), channel_id=1, source_target_pairs={{0,16},{1,17},{2,18},{3,19},{4,20},{5,21},{6,22},{7,23},{8,24},{9,... | collective-permute-start | bytes 663560 | tf_op jit(solution)/shard_map/ppermute | solution.py:78
  443.1 11.8 %collective-permute-start.41 = (bf16[880,128]{1,0:T(8,128)(2,1)S(1)}, bf16[880,128]{1,0:T(8,128)(2,1)S(1)}, u32[]{:S(2)}, u32[]{:S(2)}) collective-permute-start(bf16[880,128]{1,0:T(8,128)(2,1)S(1)} %dynamic-slice_bitcast_fusion.15), channel_id=1, source_target_pairs={{0,16},{1,17},{2,18},{3,19},{4,20},{5,21},{6,22},{7,23},{8,24},{9,... | collective-permute-start | bytes 675848 | tf_op jit(solution)/shard_map/ppermute | solution.py:78
  (46 other events, 206.3 us)

commit v2 on v1

v2 whole, which is shorter than its diff:
```python
import functools
import math

import jax
import jax.numpy as jnp
from jax import lax
from jax.experimental import pallas as pl
from jax.experimental.pallas import tpu as pltpu
from jax.sharding import PartitionSpec as P


D = 768
HD = 64
FF = 3072
LANES = 128

EPS_NORM = 1e-06
BETA_ONE = 0.9
BETA_TWO = 0.95
RATE = 0.01
DECAY = 0.05
EPS_ADAM = 1e-08
ADAM_STEP = 3.0
INV_ROOT_TWO = 0.7071067811865476
INV_ROOT_TWOPI = 0.3989422804014327
F32 = jnp.float32
BF16 = jnp.bfloat16

SEGMENTS = (
    ("g1", 1, 6),
    ("c1", 1, 6),
    ("wqkv", D, 18),
    ("bq", 1, 6),
    ("bv", 1, 6),
    ("wo", D, 6),
    ("bo", 1, 6),
    ("g2", 1, 6),
    ("c2", 1, 6),
    ("w1", D, 24),
    ("b1", 1, 24),
    ("w2", FF, 6),
    ("b2", 1, 6),
)
GROUPS = (("g1", "c1", "wqkv", "bq", "bv"), ("wo", "bo", "g2", "c2"), ("w1", "b1"), ("w2", "b2"))
OFFSETS = {}
SHAPES = {}
_at = 0
for _name, _k, _j in SEGMENTS:
    OFFSETS[_name] = _at
    SHAPES[_name] = (_k, _j)
    _at += _k * _j
USED_ROWS = _at


def round_up(value, step):
    return -(-value // step) * step


class Plan:
    def __init__(self, devices, shard):
        self.devices = devices
        self.bits = devices.bit_length() - 1
        self.rows = shard // LANES
        self.padded = round_up(self.rows, 16)
        half = round_up(self.padded // 2, 16)
        self.halves = ((0, half), (half, self.padded))
        self.quarters = 4
        self.low = devices // self.quarters
        self.low_bits = self.bits - 2

    def low_order(self, half):
        order = [1, 2] if half == 0 else [2, 1]
        return list(range(self.low_bits - 1, 2, -1)) + order + [0]


def exchange(array, mask, devices):
    return lax.ppermute(array, "fsdp", [(i, i ^ mask) for i in range(devices)])


def tie(first, second):
    return lax.optimization_barrier((first, second))


def gather_quarters(narrow, plan, me):
    quarter = me // plan.low
    result = [[None, None] for _ in range(plan.quarters)]
    high = []
    first = None
    for half, (lo, hi) in enumerate(plan.halves):
        part = narrow[None, None, lo:hi]
        if first is not None:
            first, part = tie(first, part)
        part_in = part
        other = exchange(part_in, 1 << (plan.bits - 1), plan.devices)
        if half == 0:
            first = other
        high.append([part_in, other])
    high[0][1] = first
    for half in range(2):
        part = jnp.concatenate(high[half], axis=0)
        other = exchange(part, 1 << (plan.bits - 2), plan.devices)
        part = jnp.concatenate([part, other], axis=1)
        high[half] = part.reshape((plan.quarters,) + part.shape[2:])
    for q in range(plan.quarters):
        for half in range(2):
            block = lax.dynamic_index_in_dim(high[half], quarter ^ q, 0, keepdims=False)
            block = block.reshape((1,) * (plan.low_bits - 1) + block.shape)
            for bit in plan.low_order(half):
                other = exchange(block, 1 << bit, plan.devices)
                if bit:
                    axis = plan.low_bits - 1 - bit
                    block = jnp.concatenate([block, other], axis=axis)
            shape = (plan.low // 2,) + block.shape[-2:]
            result[q][half] = (block.reshape(shape), other.reshape(shape))
    return result


def unpack_group(names, gathered, plan, position):
    start = OFFSETS[names[0]]
    stop = OFFSETS[names[-1]] + math.prod(SHAPES[names[-1]])
    first, last = start // plan.rows, (stop - 1) // plan.rows
    count = last - first + 1
    quarters = list(range(first // plan.low, last // plan.low + 1))
    flat_rows = round_up(stop - start, 8) + 8

    def kernel(*refs):
        position_ref = refs[0]
        sources = refs[1 : 1 + 4 * len(quarters)]
        outs = refs[1 + 4 * len(quarters) : -3]
        stage, flat, sems = refs[-3:]
        mine = position_ref[0]
        copies = []
        for i in range(count):
            device = first + i
            q = device // plan.low - quarters[0]
            spot = (device % plan.low) ^ mine
            for half, (lo, hi) in enumerate(plan.halves):
                for core in range(2):
                    copy = pltpu.make_async_copy(
                        sources[4 * q + 2 * half + core].at[spot // 2],
                        stage.at[i, lo:hi],
                        sems.at[i, half],
                    )
                    pl.when(spot % 2 == core)(copy.start)
                copies.append(copy)
        for i in range(count):
            copies[2 * i].wait()
            copies[2 * i + 1].wait()
            base = (first + i) * plan.rows
            row = max(start, base)
            end = min(stop, base + plan.rows)
            while row < end:
                inside = row - base
                lower = inside // 16 * 16
                upper = min(lower + 256, end - base)
                block = stage[i, lower : round_up(upper, 16), :].astype(F32)
                flat[row - start : base + upper - start, :] = block[inside - lower : upper - lower]
                row = base + upper
        for name, out in zip(names, outs):
            rows, blocks = SHAPES[name]
            offset = OFFSETS[name] - start
            if rows == 1:
                for j in range(blocks):
                    out[:, j * LANES : (j + 1) * LANES] = flat[offset + j : offset + j + 1, :]
            else:

                @pl.loop(0, blocks)
                def _(j, out=out, rows=rows, blocks=blocks, offset=offset):
                    column = flat[pl.ds(offset + j, rows, stride=blocks), :]
                    out[:, pl.ds(pl.multiple_of(j * LANES, LANES), LANES)] = column.astype(BF16)

    shapes = []
    for name in names:
        rows, blocks = SHAPES[name]
        kind = F32 if rows == 1 else BF16
        shapes.append(jax.ShapeDtypeStruct((rows, blocks * LANES), kind))
    operands = [
        gathered[q][half][core] for q in quarters for half in range(2) for core in range(2)
    ]
    results = pl.pallas_call(
        kernel,
        out_shape=shapes,
        in_specs=[pl.BlockSpec(memory_space=pltpu.SMEM)]
        + [pl.BlockSpec(memory_space=pl.ANY)] * len(operands),
        out_specs=[pl.BlockSpec(memory_space=pltpu.VMEM)] * len(shapes),
        scratch_shapes=[
            pltpu.VMEM((count, plan.padded, LANES), BF16),
            pltpu.VMEM((flat_rows, LANES), F32),
            pltpu.SemaphoreType.DMA((count, 2)),
        ],
        cost_estimate=pl.CostEstimate(
            flops=0, bytes_accessed=4 * (stop - start) * LANES, transcendentals=0
        ),
    )(position, *operands)
    return dict(zip(names, results))


def pack_quarter(quarter, factors, vectors, plan):
    start = quarter * plan.low * plan.rows
    stop = start + plan.low * plan.rows
    pieces = []
    base, top = start, stop
    for name, rows, blocks in SEGMENTS:
        offset = OFFSETS[name]
        lo, hi = max(start, offset), min(stop, offset + rows * blocks)
        if lo >= hi:
            continue
        if rows == 1:
            pieces.append((name, offset, lo - offset, hi - offset))
        else:
            k0 = (lo - offset) // blocks // LANES * LANES
            k1 = round_up(-(-(hi - offset) // blocks), LANES)
            pieces.append((name, offset, k0, k1))
            base = min(base, offset + k0 * blocks)
            top = max(top, offset + k1 * blocks)
    flat_rows = round_up(top - base, 8) + 32
    operands = []
    for name, *_ in pieces:
        operands.extend(factors[name] if name in factors else (vectors[name],))

    def kernel(*refs):
        ins = list(refs[: len(operands)])
        outs = refs[len(operands) : len(operands) + 2]
        flat, turned = refs[len(operands) + 2 :]
        for name, offset, lo, hi in pieces:
            rows, blocks = SHAPES[name]
            if rows == 1:
                row_ref = ins.pop(0)
                for j in range(lo, hi):
                    at = offset + j - base
                    flat[at : at + 1, :] = row_ref[:, j * LANES : (j + 1) * LANES]
                continue
            left, right = ins.pop(0), ins.pop(0)
            size = hi - lo
            step = 256 if size % 256 == 0 else 128
            for k in range(lo, hi, 128):
                turned[k - lo : k - lo + 128, :] = left[:, k : k + 128].T

            @pl.loop(0, blocks // 2)
            def _(pair, right=right, lo=lo, size=size, step=step, offset=offset, blocks=blocks):
                columns = right[:, pl.ds(pl.multiple_of(pair * 256, 256), 256)]

                @pl.loop(0, size // step)
                def _(part):
                    k = pl.multiple_of(part * step, step)
                    product = jnp.dot(
                        turned[pl.ds(k, step), :], columns, preferred_element_type=F32
                    )
                    at = offset - base + (lo + k) * blocks + 2 * pair
                    flat[pl.ds(at, step, stride=blocks), :] = product[:, :LANES]
                    flat[pl.ds(at + 1, step, stride=blocks), :] = product[:, LANES:]

        if stop > USED_ROWS:
            flat[max(start, USED_ROWS) - base : stop - base, :] = jnp.zeros(
                (stop - max(start, USED_ROWS), LANES), F32
            )
        for i in range(plan.low):
            for (lo, hi), out in zip(plan.halves, outs):
                for row in range(lo, hi, 256):
                    end = min(row + 256, hi)
                    at = start - base + i * plan.rows
                    out[i, row - lo : end - lo, :] = flat[at + row : at + end, :].astype(BF16)

    length = factors["w2"][0].shape[0]
    widest = max([hi - lo for name, _, lo, hi in pieces if SHAPES[name][0] > 1] + [128])
    return pl.pallas_call(
        kernel,
        out_shape=[
            jax.ShapeDtypeStruct((plan.low, hi - lo, LANES), BF16) for lo, hi in plan.halves
        ],
        in_specs=[pl.BlockSpec(memory_space=pltpu.VMEM)] * len(operands),
        out_specs=[pl.BlockSpec(memory_space=pltpu.VMEM)] * 2,
        scratch_shapes=[pltpu.VMEM((flat_rows, LANES), F32), pltpu.VMEM((widest, length), BF16)],
        cost_estimate=pl.CostEstimate(
            flops=2 * (top - base) * LANES * length,
            bytes_accessed=4 * (top - base) * LANES,
            transcendentals=0,
        ),
    )(*operands)


def halve(array, axis, bit, plan, me, last=False):
    mine = (me >> bit) & 1
    keep = lax.dynamic_index_in_dim(array, mine, axis, keepdims=False)
    send = lax.dynamic_index_in_dim(array, 1 - mine, axis, keepdims=False)
    got = exchange(send, 1 << bit, plan.devices)
    total = keep.astype(F32) + got.astype(F32)
    return total if last else total.astype(BF16)


def scatter_quarter(packed, plan, me):
    blocks = []
    for half in range(2):
        block = packed[half]
        block = block.reshape((2,) * plan.low_bits + block.shape[1:])
        left = list(range(plan.low_bits - 1, -1, -1))
        for bit in reversed(plan.low_order(half)):
            block = halve(block, left.index(bit), bit, plan, me)
            left.remove(bit)
        blocks.append(block)
    return blocks


def scatter_across(blocks, plan, me):
    parts = []
    for half in range(2):
        stacked = jnp.stack([blocks[q][half] for q in range(plan.quarters)])
        stacked = stacked.reshape((2, 2) + stacked.shape[1:])
        stacked = halve(stacked, 1, plan.bits - 2, plan, me)
        parts.append(halve(stacked, 0, plan.bits - 1, plan, me, last=True))
    return jnp.concatenate(parts, axis=0)[: plan.rows]


NT = (((1,), (1,)), ((), ()))
TN = (((0,), (0,)), ((), ()))
CHUNK = 32


def dot(left, right, numbers=(((1,), (0,)), ((), ()))):
    return lax.dot_general(left, right, numbers, preferred_element_type=F32)


def call(kernel, shapes, operands, scratch=(), scalars=0, flops=0):
    space = [pltpu.SMEM] * scalars + [pltpu.VMEM] * (len(operands) - scalars)
    moved = sum(math.prod(a.shape) * a.dtype.itemsize for a in list(operands) + list(shapes))
    return pl.pallas_call(
        kernel,
        out_shape=shapes,
        in_specs=[pl.BlockSpec(memory_space=s) for s in space],
        out_specs=[pl.BlockSpec(memory_space=pltpu.VMEM)] * len(shapes),
        scratch_shapes=list(scratch),
        cost_estimate=pl.CostEstimate(flops=flops, bytes_accessed=moved, transcendentals=0),
    )(*operands)


def array(shape, kind=F32):
    return jax.ShapeDtypeStruct(shape, kind)


def row_norm(values):
    centre = values - jnp.mean(values, axis=-1, keepdims=True)
    scale_inv = lax.rsqrt(jnp.mean(centre * centre, axis=-1, keepdims=True) + EPS_NORM)
    return centre * scale_inv, scale_inv


def row_norm_back(grad, values, gain):
    normed, scale_inv = row_norm(values)
    scaled = grad * gain
    back = scale_inv * (
        scaled
        - jnp.mean(scaled, axis=-1, keepdims=True)
        - normed * jnp.mean(scaled * normed, axis=-1, keepdims=True)
    )
    return back, jnp.sum(grad * normed, axis=0, keepdims=True)


def rows_of(index, size=CHUNK):
    return pl.ds(pl.multiple_of(index * size, size), size)


def fill_padded(target, source, stride):
    slots, tokens, _ = source.shape
    target[...] = jnp.zeros_like(target)
    for s in range(slots):
        target[s * stride : s * stride + tokens, :] = source[s]


def fill_masked(target, source, count, stride):
    slots, tokens, _ = source.shape
    target[...] = jnp.zeros_like(target)
    for s in range(slots):
        live = jnp.where(s < count, 1.0, 0.0).astype(F32)
        target[s * stride : s * stride + tokens, :] = source[s] * live


def run_block(counts, inputs, cotangent, w, pack):
    slots, tokens, _ = inputs.shape
    stride = round_up(tokens, 16)
    total = slots * stride
    heads = D // HD
    pairs = heads // 2
    qk_scale = 1.0 / math.sqrt(HD)

    def head_rows(i):
        return pl.ds(pl.multiple_of(i // pairs * stride, 16), stride)

    def head_columns(i, part):
        return pl.ds(pl.multiple_of(part * D + i % pairs * LANES, LANES), LANES)

    def lane_mask(part):
        lane = lax.broadcasted_iota(jnp.int32, (stride, LANES), 1)
        return (lane < HD) if part == 0 else (lane >= HD)

    def attend(count, x, cot, g1, c1, wqkv, bq, bv, a1, qkv, weights, mixed, narrow, gb2, padded):
        fill_masked(padded, cot, count[0], stride)
        gb2[...] = jnp.sum(padded[...], axis=0, keepdims=True)
        narrow[...] = padded[...].astype(BF16)
        fill_padded(padded, x, stride)

        @pl.loop(0, total // CHUNK)
        def _(i):
            normed, _ = row_norm(padded[rows_of(i), :])
            a1[rows_of(i), :] = (normed * g1[...] + c1[...]).astype(BF16)

        qkv[:, :D] = (dot(a1[...], wqkv[:, :D]) + bq[...]).astype(BF16)
        qkv[:, D : 2 * D] = dot(a1[...], wqkv[:, D : 2 * D]).astype(BF16)
        qkv[:, 2 * D :] = (dot(a1[...], wqkv[:, 2 * D :]) + bv[...]).astype(BF16)
        hidden = lax.broadcasted_iota(jnp.int32, (stride, stride), 1) >= tokens

        @pl.loop(0, slots * pairs)
        def _(i):
            query = qkv[head_rows(i), head_columns(i, 0)]
            key = qkv[head_rows(i), head_columns(i, 1)]
            value = qkv[head_rows(i), head_columns(i, 2)]
            outs = []
            for part in range(2):
                masked = jnp.where(lane_mask(part), query, jnp.zeros_like(query))
                scores = dot(masked, key, NT) * qk_scale
                scores = jnp.where(hidden, -1e30, scores)
                top = jnp.max(scores, axis=-1, keepdims=True)
                log_total = top + jnp.log(
                    jnp.sum(jnp.exp(scores - top), axis=-1, keepdims=True)
                )
                soft = jnp.exp(scores - log_total)
                weights[2 * i + part] = soft
                outs.append(dot(soft.astype(BF16), value))
            mixed[head_rows(i), head_columns(i, 0)] = jnp.where(
                lane_mask(0), outs[0], outs[1]
            ).astype(BF16)

    a1, qkv, weights, mixed, narrow, gb2 = call(
        attend,
        [
            array((total, D), BF16),
            array((total, 3 * D), BF16),
            array((slots * heads, stride, stride)),
            array((total, D), BF16),
            array((total, D), BF16),
            array((1, D)),
        ],
        [counts, inputs, cotangent, w["g1"], w["c1"], w["wqkv"], w["bq"], w["bv"]],
        [pltpu.VMEM((total, D), F32)],
        scalars=1,
        flops=8 * total * D * D,
    )

    width = 512

    def widen(x, mixed, wo, bo, g2, c2, w1, b1, middle, a2, rows, slope, block):
        fill_padded(middle, x, stride)
        middle[...] = middle[...] + (dot(mixed[...], wo[...]) + bo[...])

        @pl.loop(0, total // CHUNK)
        def _(i):
            normed, _ = row_norm(middle[rows_of(i), :])
            a2[rows_of(i), :] = (normed * g2[...] + c2[...]).astype(BF16)

        @pl.loop(0, FF // width)
        def _(j):
            columns = rows_of(j, width)
            block[...] = dot(a2[...], w1[:, columns]) + b1[:, columns]

            @pl.loop(0, total // CHUNK)
            def _(i):
                value = block[rows_of(i), :]
                phi = 0.5 * (1.0 + lax.erf(value * INV_ROOT_TWO))
                rows[rows_of(i), columns] = (value * phi).astype(BF16)
                slope[rows_of(i), columns] = (
                    phi + value * jnp.exp(-0.5 * value * value) * INV_ROOT_TWOPI
                )

    middle, a2, rows, slope = call(
        widen,
        [
            array((total, D)),
            array((total, D), BF16),
            array((total, FF), BF16),
            array((total, FF)),
        ],
        [inputs, mixed, w["wo"], w["bo"], w["g2"], w["c2"], w["w1"], w["b1"]],
        [pltpu.VMEM((total, width), F32)],
        flops=10 * total * D * D,
    )
    factors = {"w2": (rows, narrow)}
    vectors = {"b2": gb2}
    narrow = pack(3, factors, vectors, narrow)

    def finish(middle, rows, slope, narrow, w2, b2, out, d_pre, gb1):
        final = middle[...] + (dot(rows[...], w2[...]) + b2[...])
        for s in range(slots):
            out[s] = final[s * stride : s * stride + tokens, :]

        @pl.loop(0, FF // width)
        def _(j):
            columns = rows_of(j, width)
            grad = dot(narrow[...], w2[columns, :], NT) * slope[:, columns]
            d_pre[:, columns] = grad.astype(BF16)
            gb1[:, columns] = jnp.sum(grad, axis=0, keepdims=True)

    outputs, d_pre, gb1 = call(
        finish,
        [array(inputs.shape), array((total, FF), BF16), array((1, FF))],
        [middle, rows, slope, narrow, w["w2"], w["b2"]],
        flops=16 * total * D * D,
    )
    factors["w1"] = (a2, d_pre)
    vectors["b1"] = gb1
    d_pre = pack(2, factors, vectors, d_pre)

    def back_middle(
        count, cot, middle, d_pre, w1, wo, g2, d_mid, d_narrow, d_mixed, gg2, gc2, gbo, work
    ):
        work[...] = dot(d_pre[...], w1[...], NT)
        gc2[...] = jnp.sum(work[...], axis=0, keepdims=True)
        gg2[...] = jnp.zeros_like(gg2)
        fill_masked(d_mid, cot, count[0], stride)

        @pl.loop(0, total // CHUNK)
        def _(i):
            back, gain = row_norm_back(work[rows_of(i), :], middle[rows_of(i), :], g2[...])
            gg2[...] += gain
            grad = d_mid[rows_of(i), :] + back
            d_mid[rows_of(i), :] = grad
            d_narrow[rows_of(i), :] = grad.astype(BF16)

        gbo[...] = jnp.sum(d_mid[...], axis=0, keepdims=True)
        d_mixed[...] = dot(d_narrow[...], wo[...], NT).astype(BF16)

    d_mid, d_narrow, d_mixed, gg2, gc2, gbo = call(
        back_middle,
        [
            array((total, D)),
            array((total, D), BF16),
            array((total, D), BF16),
            array((1, D)),
            array((1, D)),
            array((1, D)),
        ],
        [counts, cotangent, middle, d_pre, w["w1"], w["wo"], w["g2"]],
        [pltpu.VMEM((total, D), F32)],
        scalars=1,
        flops=10 * total * D * D,
    )
    factors["wo"] = (mixed, d_narrow)
    vectors.update(bo=gbo, g2=gg2, c2=gc2)
    d_mixed = pack(1, factors, vectors, d_mixed)

    def back_attend(
        x, qkv, weights, d_mixed, d_mid, wqkv, g1, d_proj, grad_in, gbq, gbv, gg1, gc1, padded, work
    ):
        gbq[...] = jnp.zeros_like(gbq)
        gbv[...] = jnp.zeros_like(gbv)

        @pl.loop(0, slots * pairs)
        def _(i):
            query = qkv[head_rows(i), head_columns(i, 0)]
            key = qkv[head_rows(i), head_columns(i, 1)]
            value = qkv[head_rows(i), head_columns(i, 2)]
            grad = d_mixed[head_rows(i), head_columns(i, 0)]
            found = []
            for part in range(2):
                soft = weights[2 * i + part]
                masked = jnp.where(lane_mask(part), grad, jnp.zeros_like(grad))
                d_soft = dot(masked, value, NT)
                row_dot = jnp.sum(soft * d_soft, axis=-1, keepdims=True)
                d_scores = (soft * (d_soft - row_dot) * qk_scale).astype(BF16)
                found.append(
                    (
                        dot(d_scores, key),
                        dot(d_scores, query, TN),
                        dot(soft.astype(BF16), grad, TN),
                    )
                )
            joined = [jnp.where(lane_mask(0), a, b) for a, b in zip(*found)]
            for part in range(3):
                d_proj[head_rows(i), head_columns(i, part)] = joined[part].astype(BF16)
            gbq[:, head_columns(i, 0)] += jnp.sum(joined[0], axis=0, keepdims=True)
            gbv[:, head_columns(i, 0)] += jnp.sum(joined[2], axis=0, keepdims=True)

        work[...] = dot(d_proj[...], wqkv[...], NT)
        gc1[...] = jnp.sum(work[...], axis=0, keepdims=True)
        gg1[...] = jnp.zeros_like(gg1)
        fill_padded(padded, x, stride)

        @pl.loop(0, total // CHUNK)
        def _(i):
            back, gain = row_norm_back(work[rows_of(i), :], padded[rows_of(i), :], g1[...])
            gg1[...] += gain
            work[rows_of(i), :] = d_mid[rows_of(i), :] + back

        for s in range(slots):
            grad_in[s] = work[s * stride : s * stride + tokens, :]

    d_proj, input_grad, gbq, gbv, gg1, gc1 = call(
        back_attend,
        [
            array((total, 3 * D), BF16),
            array(inputs.shape),
            array((1, D)),
            array((1, D)),
            array((1, D)),
            array((1, D)),
        ],
        [inputs, qkv, weights, d_mixed, d_mid, w["wqkv"], w["g1"]],
        [pltpu.VMEM((total, D), F32)] * 2,
        flops=8 * total * D * D,
    )
    factors["wqkv"] = (a1, d_proj)
    vectors.update(bq=gbq, bv=gbv, g1=gg1, c1=gc1)
    pack(0, factors, vectors, d_proj)
    return outputs, input_grad


def adam_update(params, grads, moment_one, moment_two):
    new_one = BETA_ONE * moment_one + (1.0 - BETA_ONE) * grads
    new_two = BETA_TWO * moment_two + (1.0 - BETA_TWO) * grads * grads
    fix_one = 1.0 - BETA_ONE**ADAM_STEP
    fix_two = 1.0 - BETA_TWO**ADAM_STEP
    update = new_one / fix_one / (jnp.sqrt(new_two / fix_two) + EPS_ADAM)
    return (params - RATE * (update + DECAY * params), new_one, new_two)


def local(plan, *operands):
    return layer_step(plan, *operands)


def layer_step(plan, inputs, cotangent, counts, params, moment_one, moment_two):
    me = lax.axis_index("fsdp")
    rows = params.reshape(plan.rows, LANES)
    narrow = jnp.pad(rows.astype(BF16), ((0, plan.padded - plan.rows), (0, 0)))
    gathered = gather_quarters(narrow, plan, me)
    position = (me % plan.low).astype(jnp.int32).reshape(1)
    weights = {}
    for names in GROUPS:
        weights.update(unpack_group(names, gathered, plan, position))
    summed = {}

    def pack(q, factors, vectors, after):
        packed = pack_quarter(q, factors, vectors, plan)
        packed, after = tie(packed, after)
        summed[q] = scatter_quarter(packed, plan, me)
        return after

    outputs, input_grad = run_block(counts, inputs, cotangent, weights, pack)
    shard_grad = scatter_across(summed, plan, me)
    new_params, new_one, new_two = adam_update(
        rows,
        shard_grad,
        moment_one.reshape(plan.rows, LANES),
        moment_two.reshape(plan.rows, LANES),
    )
    flat = lambda array: array.reshape(-1)
    return (outputs, input_grad, flat(shard_grad), flat(new_params), flat(new_one), flat(new_two))


def solution(mesh):
    devices = mesh.shape["fsdp"]

    def step(inputs, cotangent, counts, params, moment_one, moment_two):
        plan = Plan(devices, params.shape[0] // devices)
        placed = (P("fsdp", None, None),) * 2 + (P("fsdp"),) * 4
        return jax.shard_map(
            functools.partial(local, plan),
            mesh=mesh,
            in_specs=placed,
            out_specs=placed,
            check_vma=False,
        )(inputs, cotangent, counts, params, moment_one, moment_two)

    return step
```

time: 464 us -> 392 us (0.84); the launches traced: 458 us -> 391 us
  Pallas kernels: 71.9 us -> 143 us
  matrix products: 60.8 us -> 0 us
  local copies, waits for them, and re-layouts: 63 us -> 19.5 us
  other arithmetic: 47.7 us -> 11.8 us
    pallas_call x0 -> x5, Pallas kernels: none -> 72.6 us  [call(): pl.pallas_call(kernel, out_shape=shapes, in_specs=[pl.BlockSpec(memory_sp...]
    dot_general x14 -> x0, matrix products: 60.8 us -> none  [the longest x6 26.9 us: batched(): return jnp.einsum(form, left, right, preferred_element_type=F32)]
    reshape x30 -> x2, local copies, waits for them, and re-layouts: 32.2 us -> 0.15 us  [gather_quarters(): block = block.reshape((1,) * (plan.low_bits - 1) + block.shape)]
    concatenate x28 -> x19, other arithmetic: 19.3 us -> 3.24 us  [the longest x16 3.02 us: gather_quarters(): block = jnp.concatenate([block, other], axis=axis)]
    reduce_sum x10 -> x0, other arithmetic: 9.25 us -> none  [the longest x1 3.79 us: run_block(): jnp.sum(d_mid_rows, axis=0)]
    pad x8 -> x0, local copies, waits for them, and re-layouts: 9.1 us -> none  [run_block(): pad = lambda rows: jnp.pad(rows, ((0, TPAD - row_count), (0, 0)))]
    unnamed x112 -> x51, local copies, waits for them, and re-layouts: 6.21 us -> 13.8 us
    dynamic_slice x2, local copies, waits for them, and re-layouts: 6.02 us -> 0.35 us  [halve(): keep = lax.dynamic_index_in_dim(array, mine, axis, keepdims=False)]
  transfers between devices with their start and end apart: 56 -> 56, of which waited for: 26 -> 29; matrix products, arithmetic and copies ran while one was open for 10% -> 5% of each run, Pallas kernels for 12% -> 15%
where the time goes in v2:
time: 392 us; the launch traced here: 391 us
  waiting for transfers between devices  163 us (42%)
  Pallas kernels  143 us (36%)
  starting transfers between devices  51.8 us (13%)
  local copies, waits for them, and re-layouts  19.5 us (5%)
  other arithmetic  11.8 us (3%)
    ppermute x56, waiting for transfers between devices, exchange(): return lax.ppermute(array, 'fsdp', [(i, i ^ mask) for i in range(devices)])  163 us
    pallas_call x5, Pallas kernels, call(): pl.pallas_call(kernel, out_shape=shapes, in_specs=[pl.BlockSpec(memory_sp...  72.6 us
    ppermute x56, starting transfers between devices, exchange(): return lax.ppermute(array, 'fsdp', [(i, i ^ mask) for i in range(devices)])  51.8 us
    pallas_call x4, Pallas kernels, pack_quarter(): pl.pallas_call(kernel, out_shape=[jax.ShapeDtypeStruct((plan.low, hi - lo...  49.2 us
    pallas_call x4, Pallas kernels, unpack_group(): pl.pallas_call(kernel, out_shape=shapes, in_specs=[pl.BlockSpec(memory_sp...  21.3 us
    unnamed x51, local copies, waits for them, and re-layouts  13.8 us
  transfers between devices with their start and end apart: 56, of which 29 were waited for; matrix products, arithmetic and copies ran while one was open for 5% of the time, Pallas kernels for 15%

profile of v2, /device:TPU:0, one launch (start us, length us, event | category | flops | bytes accessed | tf_op | source)
XLA Modules:
  0.0 391.2 jit_solution(8273273107578860668)
XLA Ops:
  1.9 4.1 %collective-permute-start = (bf16[1,1,880,128]{3,2,1,0:T(8,128)(2,1)S(1)}, bf16[1,1,880,128]{3,2,1,0:T(8,128)(2,1)S(1)}, u32[]{:S(2)}, u32[]{:S(2)}) collective-permute-start(bf16[1,1,880,128]{3,2,1,0:T(8,128)(2,1)S(1)} %slice_bitcast_fusion), channel_id=1, source_target_pairs={{0,16},{1,17},{2,18},{3,19},{4,20},{5,21},{6,22},{7,23},{8,24},{9,... | collective-permute-start | bytes 675848 | tf_op jit(solution)/shard_map/ppermute | solution.py:77
  6.0 10.3 %collective-permute-done = bf16[1,1,880,128]{3,2,1,0:T(8,128)(2,1)S(1)} collective-permute-done((bf16[1,1,880,128]{3,2,1,0:T(8,128)(2,1)S(1)}, bf16[1,1,880,128]{3,2,1,0:T(8,128)(2,1)S(1)}, u32[]{:S(2)}, u32[]{:S(2)}) %collective-permute-start) | collective-permute-done | bytes 225312 | tf_op jit(solution)/shard_map/ppermute | solution.py:77
  16.4 4.2 %collective-permute-start.1 = (bf16[2,1,880,128]{3,2,1,0:T(8,128)(2,1)S(1)}, bf16[2,1,880,128]{3,2,1,0:T(8,128)(2,1)S(1)}, u32[]{:S(2)}, u32[]{:S(2)}) collective-permute-start(bf16[2,1,880,128]{3,2,1,0:T(8,128)(2,1)S(1)} %pad_maximum_fusion.13), channel_id=1, source_target_pairs={{0,8},{1,9},{2,10},{3,11},{4,12},{5,13},{6,14},{7,15},{8,0},{9,1},... | collective-permute-start | bytes 1351688 | tf_op jit(solution)/shard_map/ppermute | solution.py:77
  20.6 8.1 %collective-permute-done.5 = bf16[1,1,864,128]{3,2,1,0:T(8,128)(2,1)S(1)} collective-permute-done((bf16[1,1,864,128]{3,2,1,0:T(8,128)(2,1)S(1)}, bf16[1,1,864,128]{3,2,1,0:T(8,128)(2,1)S(1)}, u32[]{:S(2)}, u32[]{:S(2)}) %collective-permute-start.5) | collective-permute-done | bytes 221216 | tf_op jit(solution)/shard_map/ppermute | solution.py:77
  28.8 5.9 %collective-permute-done.1 = bf16[2,1,880,128]{3,2,1,0:T(8,128)(2,1)S(1)} collective-permute-done((bf16[2,1,880,128]{3,2,1,0:T(8,128)(2,1)S(1)}, bf16[2,1,880,128]{3,2,1,0:T(8,128)(2,1)S(1)}, u32[]{:S(2)}, u32[]{:S(2)}) %collective-permute-start.1) | collective-permute-done | bytes 450592 | tf_op jit(solution)/shard_map/ppermute | solution.py:77
  34.9 1.3 collective-permute-start.16
  37.0 1.3 collective-permute-start.10
  39.0 4.2 %collective-permute-done.6 = bf16[2,1,864,128]{3,2,1,0:T(8,128)(2,1)S(1)} collective-permute-done((bf16[2,1,864,128]{3,2,1,0:T(8,128)(2,1)S(1)}, bf16[2,1,864,128]{3,2,1,0:T(8,128)(2,1)S(1)}, u32[]{:S(2)}, u32[]{:S(2)}) %collective-permute-start.6) | collective-permute-done | bytes 442400 | tf_op jit(solution)/shard_map/ppermute | solution.py:77
  43.4 1.4 collective-permute-start.25
  45.6 2.6 collective-permute-done.22
  48.2 1.3 collective-permute-start.13
  49.6 3.1 collective-permute-done.10
  52.7 1.3 collective-permute-start.17
  55.1 1.3 collective-permute-start.11
  56.5 1.3 collective-permute-start.7
  57.9 3.4 collective-permute-done.13
  61.3 1.3 collective-permute-start.23
  63.4 7.5 %collective-permute-done.17 = bf16[1,2,880,128]{3,2,1,0:T(8,128)(2,1)S(1)} collective-permute-done((bf16[1,2,880,128]{3,2,1,0:T(8,128)(2,1)S(1)}, bf16[1,2,880,128]{3,2,1,0:T(8,128)(2,1)S(1)}, u32[]{:S(2)}, u32[]{:S(2)}) %collective-permute-start.17) | collective-permute-done | bytes 450592 | tf_op jit(solution)/shard_map/ppermute | solution.py:77
  72.3 13.0 %collective-permute-done.7 = bf16[1,1,864,128]{3,2,1,0:T(8,128)(2,1)S(1)} collective-permute-done((bf16[1,1,864,128]{3,2,1,0:T(8,128)(2,1)S(1)}, bf16[1,1,864,128]{3,2,1,0:T(8,128)(2,1)S(1)}, u32[]{:S(2)}, u32[]{:S(2)}) %collective-permute-start.7) | collective-permute-done | bytes 221216 | tf_op jit(solution)/shard_map/ppermute | solution.py:77
  85.3 1.3 collective-permute-start.20
  86.8 8.2 %collective-permute-done.23 = bf16[1,2,880,128]{3,2,1,0:T(8,128)(2,1)S(1)} collective-permute-done((bf16[1,2,880,128]{3,2,1,0:T(8,128)(2,1)S(1)}, bf16[1,2,880,128]{3,2,1,0:T(8,128)(2,1)S(1)}, u32[]{:S(2)}, u32[]{:S(2)}) %collective-permute-start.23) | collective-permute-done | bytes 450592 | tf_op jit(solution)/shard_map/ppermute | solution.py:77
  95.0 7.8 %collective-permute-done.3 = bf16[1,2,880,128]{3,2,1,0:T(8,128)(2,1)S(1)} collective-permute-done((bf16[1,2,880,128]{3,2,1,0:T(8,128)(2,1)S(1)}, bf16[1,2,880,128]{3,2,1,0:T(8,128)(2,1)S(1)}, u32[]{:S(2)}, u32[]{:S(2)}) %collective-permute-start.3) | collective-permute-done | bytes 450592 | tf_op jit(solution)/shard_map/ppermute | solution.py:77
  102.8 1.3 collective-permute-start.26
  106.3 9.6 %collective-permute-done.26 = bf16[2,1,864,128]{3,2,1,0:T(8,128)(2,1)S(1)} collective-permute-done((bf16[2,1,864,128]{3,2,1,0:T(8,128)(2,1)S(1)}, bf16[2,1,864,128]{3,2,1,0:T(8,128)(2,1)S(1)}, u32[]{:S(2)}, u32[]{:S(2)}) %collective-permute-start.26) | collective-permute-done | bytes 442400 | tf_op jit(solution)/shard_map/ppermute | solution.py:77
  115.9 6.8 %collective-permute-done.8 = bf16[2,1,864,128]{3,2,1,0:T(8,128)(2,1)S(1)} collective-permute-done((bf16[2,1,864,128]{3,2,1,0:T(8,128)(2,1)S(1)}, bf16[2,1,864,128]{3,2,1,0:T(8,128)(2,1)S(1)}, u32[]{:S(2)}, u32[]{:S(2)}) %collective-permute-start.8) | collective-permute-done | bytes 442400 | tf_op jit(solution)/shard_map/ppermute | solution.py:77
  126.5 2.2 copy.14.x
  130.4 3.0 shard_map.111
  133.4 7.6 %shard_map.112 = (bf16[768,3072]{1,0:T(8,128)(2,1)}, f32[1,3072]{1,0:T(1,128)}) custom-call(s32[1]{0:T(128)} %bitcast.refs_0_, bf16[4,880,128]{2,1,0:T(8,128)(2,1)} %bitcast.255, bf16[4,880,128]{2,1,0:T(8,128)(2,1)} %bitcast.264, bf16[4,864,128]{2,1,0:T(8,128)(2,1)} %bitcast.259, bf16[4,864,128]{2,1,0:T(8,128)(2,1)} %bitcast.273, ...), custom_call_target="tpu_custom_call" | custom-call | bytes 9449472 | tf_op jit(solution)/shard_map/pallas_call | solution.py:180
  141.0 4.9 %shard_map.109 = (f32[1,768]{1,0:T(1,128)}, f32[1,768]{1,0:T(1,128)}, bf16[768,2304]{1,0:T(8,128)(2,1)}, f32[1,768]{1,0:T(1,128)}, f32[1,768]{1,0:T(1,128)}) custom-call(s32[1]{0:T(128)} %bitcast.refs_0_, bf16[4,880,128]{2,1,0:T(8,128)(2,1)} %bitcast.6.refs_1_, bf16[4,880,128]{2,1,0:T(8,128)(2,1)} %bitcast.7.refs_2_, bf16[4,864,128]{2,1,0:T(8,128)(2,1)} %bitcast.10.refs_3_, ...), custom_call_target="tpu_custom_call" | custom-call | bytes 7090176 | tf_op jit(solution)/shard_map/pallas_call | solution.py:180
  145.9 18.3 %shard_map.110 = (bf16[320,768]{1,0:T(8,128)(2,1)}, bf16[320,2304]{1,0:T(8,128)(2,1)}, f32[24,160,160]{2,1,0:T(8,128)}, bf16[320,768]{1,0:T(8,128)(2,1)}, bf16[320,768]{1,0:T(8,128)(2,1)}, /*index=5*/f32[1,768]{1,0:T(1,128)}) custom-call(s32[1]{0:T(128)S(6)} %copy.50.count, f32[2,145,768]{2,1,0:T(8,128)} %copy.14.x, f32[2,145,768]{2,1,0:T(8,128)} %copy.13.cot, ...), custom_call_target="tpu_custom_call" | custom-call | flops 1509949440 | bytes 10742788 | tf_op jit(solution)/shard_map/pallas_call | solution.py:326
  164.2 13.3 %shard_map.113 = (f32[320,768]{1,0:T(8,128)}, bf16[320,768]{1,0:T(8,128)(2,1)}, bf16[320,3072]{1,0:T(8,128)(2,1)}, f32[320,3072]{1,0:T(8,128)}) custom-call(f32[2,145,768]{2,1,0:T(8,128)} %copy.14.x, bf16[320,768]{1,0:T(8,128)(2,1)} %get-tuple-element.72.mixed.refs_0_, bf16[768,768]{1,0:T(8,128)(2,1)} %get-tuple-element.73.wo, ...), custom_call_target="tpu_custom_call" | custom-call | flops 1887436800 | bytes 14674944 | tf_op jit(solution)/shard_map/pallas_call | solution.py:326
  177.5 10.8 %shard_map.114 = (bf16[8,880,128]{2,1,0:T(8,128)(2,1)}, bf16[8,864,128]{2,1,0:T(8,128)(2,1)}) custom-call(bf16[320,3072]{1,0:T(8,128)(2,1)} %get-tuple-element.80.refs_0_.rows.refs_3_, bf16[320,768]{1,0:T(8,128)(2,1)} %get-tuple-element.86.refs_1_.narrow.refs_4_, f32[1,768]{1,0:T(1,128)} %get-tuple-element.83.refs_2_), custom_call_target="tpu_custom_call" | custom-call | flops 1134919680 | bytes 7093248 | tf_op jit(solution)/shard_map/pallas_call | solution.py:266
  189.2 5.8 %shard_map.115 = (bf16[3072,768]{1,0:T(8,128)(2,1)}, f32[1,768]{1,0:T(1,128)}) custom-call(s32[1]{0:T(128)} %bitcast.refs_0_, bf16[4,880,128]{2,1,0:T(8,128)(2,1)} %bitcast.253, bf16[4,880,128]{2,1,0:T(8,128)(2,1)} %bitcast.261, bf16[4,864,128]{2,1,0:T(8,128)(2,1)} %bitcast.257, bf16[4,864,128]{2,1,0:T(8,128)(2,1)} %bitcast.23.refs_8_.refs_4_, ...), custom_call_target="tpu_custom_call" | custom-call | bytes 9440256 | tf_op jit(solution)/shard_map/pallas_call | solution.py:180
  195.0 10.3 %shard_map.116 = (f32[2,145,768]{2,1,0:T(8,128)}, bf16[320,3072]{1,0:T(8,128)(2,1)}, f32[1,3072]{1,0:T(1,128)}) custom-call(f32[320,768]{1,0:T(8,128)} %get-tuple-element.79.middle, bf16[320,3072]{1,0:T(8,128)(2,1)} %get-tuple-element.80.refs_0_.rows.refs_3_, f32[320,3072]{1,0:T(8,128)} %get-tuple-element.81.slope, ...), custom_call_target="tpu_custom_call" | custom-call | flops 3019898880 | bytes 14963712 | tf_op jit(solution)/shard_map/pallas_call | solution.py:326
  205.3 16.2 %shard_map.117 = (bf16[8,880,128]{2,1,0:T(8,128)(2,1)}, bf16[8,864,128]{2,1,0:T(8,128)(2,1)}) custom-call(bf16[320,768]{1,0:T(8,128)(2,1)} %get-tuple-element.92.refs_0_.refs_5_, bf16[320,3072]{1,0:T(8,128)(2,1)} %get-tuple-element.97.refs_1_.d_pre.refs_6_, f32[1,3072]{1,0:T(1,128)} %get-tuple-element.94.refs_2_, ...), custom_call_target="tpu_custom_call" | custom-call | flops 1197342720 | bytes 7483392 | tf_op jit(solution)/shard_map/pallas_call | solution.py:266
  221.5 10.6 %shard_map.118 = (f32[320,768]{1,0:T(8,128)}, bf16[320,768]{1,0:T(8,128)(2,1)}, bf16[320,768]{1,0:T(8,128)(2,1)}, f32[1,768]{1,0:T(1,128)}, f32[1,768]{1,0:T(1,128)}, /*index=5*/f32[1,768]{1,0:T(1,128)}) custom-call(s32[1]{0:T(128)S(6)} %copy.50.count, f32[2,145,768]{2,1,0:T(8,128)} %copy.13.cot, f32[320,768]{1,0:T(8,128)} %get-tuple-element.79.middle, ...), custom_call_target="tpu_custom_call" | custom-call | flops 1887436800 | bytes 11716612 | tf_op jit(solution)/shard_map/pallas_call | solution.py:326
  232.2 12.1 %shard_map.119 = (bf16[8,880,128]{2,1,0:T(8,128)(2,1)}, bf16[8,864,128]{2,1,0:T(8,128)(2,1)}) custom-call(bf16[320,768]{1,0:T(8,128)(2,1)} %get-tuple-element.72.mixed.refs_0_, bf16[320,768]{1,0:T(8,128)(2,1)} %get-tuple-element.98.refs_1_, f32[1,768]{1,0:T(1,128)} %get-tuple-element.99.refs_2_, f32[1,768]{1,0:T(1,128)} %get-tuple-element.100.refs_3_, ...), custom_call_target="tpu_custom_call" | custom-call | flops 1385594880 | bytes 8659968 | tf_op jit(solution)/shard_map/pallas_call | solution.py:266
  244.3 20.0 %shard_map.120 = (bf16[320,2304]{1,0:T(8,128)(2,1)}, f32[2,145,768]{2,1,0:T(8,128)}, f32[1,768]{1,0:T(1,128)}, f32[1,768]{1,0:T(1,128)}, f32[1,768]{1,0:T(1,128)}, /*index=5*/f32[1,768]{1,0:T(1,128)}) custom-call(f32[2,145,768]{2,1,0:T(8,128)} %copy.14.x, bf16[320,2304]{1,0:T(8,128)(2,1)} %get-tuple-element.90.qkv, ...), custom_call_target="tpu_custom_call" | custom-call | flops 1509949440 | bytes 12217344 | tf_op jit(solution)/shard_map/pallas_call | solution.py:326
  264.3 10.1 %shard_map.121 = (bf16[8,880,128]{2,1,0:T(8,128)(2,1)}, bf16[8,864,128]{2,1,0:T(8,128)(2,1)}) custom-call(f32[1,768]{1,0:T(1,128)} %get-tuple-element.108.refs_0_, f32[1,768]{1,0:T(1,128)} %get-tuple-element.109.refs_1_, bf16[320,768]{1,0:T(8,128)(2,1)} %get-tuple-element.110.refs_2_, bf16[320,2304]{1,0:T(8,128)(2,1)} %get-tuple-element.111.refs_3_, ...), custom_call_target="tpu_custom_call" | custom-call | flops 1134428160 | bytes 7090176 | tf_op jit(solution)/shard_map/pallas_call | solution.py:266
  274.4 1.4 dynamic-slice_bitcast_fusion.4
  285.1 1.3 collective-permute-start.43
  290.9 1.6 collective-permute-start.29
  292.8 5.3 %collective-permute-done.43 = bf16[2,864,128]{2,1,0:T(8,128)(2,1)S(1)} collective-permute-done((bf16[2,864,128]{2,1,0:T(8,128)(2,1)S(1)}, bf16[2,864,128]{2,1,0:T(8,128)(2,1)S(1)}, u32[]{:S(2)}, u32[]{:S(2)}) %collective-permute-start.43) | collective-permute-done | bytes 442400 | tf_op jit(solution)/shard_map/ppermute | solution.py:77
  298.2 1.3 collective-permute-start.32
  299.6 8.0 %collective-permute-done.46 = bf16[2,864,128]{2,1,0:T(8,128)(2,1)S(1)} collective-permute-done((bf16[2,864,128]{2,1,0:T(8,128)(2,1)S(1)}, bf16[2,864,128]{2,1,0:T(8,128)(2,1)S(1)}, u32[]{:S(2)}, u32[]{:S(2)}) %collective-permute-start.46) | collective-permute-done | bytes 442400 | tf_op jit(solution)/shard_map/ppermute | solution.py:77
  307.7 1.3 collective-permute-start.35
  309.2 8.0 %collective-permute-done.49 = bf16[2,864,128]{2,1,0:T(8,128)(2,1)S(1)} collective-permute-done((bf16[2,864,128]{2,1,0:T(8,128)(2,1)S(1)}, bf16[2,864,128]{2,1,0:T(8,128)(2,1)S(1)}, u32[]{:S(2)}, u32[]{:S(2)}) %collective-permute-start.49) | collective-permute-done | bytes 442400 | tf_op jit(solution)/shard_map/ppermute | solution.py:77
  317.1 1.3 collective-permute-start.38
  318.6 7.4 %collective-permute-done.52 = bf16[2,864,128]{2,1,0:T(8,128)(2,1)S(1)} collective-permute-done((bf16[2,864,128]{2,1,0:T(8,128)(2,1)S(1)}, bf16[2,864,128]{2,1,0:T(8,128)(2,1)S(1)}, u32[]{:S(2)}, u32[]{:S(2)}) %collective-permute-start.52) | collective-permute-done | bytes 442400 | tf_op jit(solution)/shard_map/ppermute | solution.py:77
  326.0 1.3 collective-permute-start.44
  328.4 1.4 collective-permute-start.50
  330.9 2.2 collective-permute-done.38
  334.3 3.6 collective-permute-done.44
  338.9 3.7 collective-permute-done.47
  343.6 3.7 collective-permute-done.50
  348.4 2.2 collective-permute-done.53
  351.8 1.8 collective-permute-done.39
  354.9 2.6 copy.27
  357.4 1.4 copy.26
  358.8 6.1 %collective-permute-done.54 = bf16[2,864,128]{2,1,0:T(8,128)(2,1)} collective-permute-done((bf16[2,864,128]{2,1,0:T(8,128)(2,1)}, bf16[2,864,128]{2,1,0:T(8,128)(2,1)}, u32[]{:S(2)}, u32[]{:S(2)}) %collective-permute-start.54) | collective-permute-done | bytes 442400 | tf_op jit(solution)/shard_map/ppermute | solution.py:77
  366.1 2.8 collective-permute-start.55
  368.9 7.9 %collective-permute-done.40 = bf16[2,880,128]{2,1,0:T(8,128)(2,1)S(1)} collective-permute-done((bf16[2,880,128]{2,1,0:T(8,128)(2,1)}, bf16[2,880,128]{2,1,0:T(8,128)(2,1)S(1)}, u32[]{:S(2)}, u32[]{:S(2)}) %collective-permute-start.40) | collective-permute-done | bytes 450592 | tf_op jit(solution)/shard_map/ppermute | solution.py:77
  377.7 11.0 %collective-permute-done.41 = bf16[880,128]{1,0:T(8,128)(2,1)S(1)} collective-permute-done((bf16[880,128]{1,0:T(8,128)(2,1)S(1)}, bf16[880,128]{1,0:T(8,128)(2,1)S(1)}, u32[]{:S(2)}, u32[]{:S(2)}) %collective-permute-start.41) | collective-permute-done | bytes 225312 | tf_op jit(solution)/shard_map/ppermute | solution.py:77
  388.8 2.4 fusion.41
  (198 shorter events, 40.7 us)
Async XLA Ops:
  1.9 14.5 %collective-permute-start = (bf16[1,1,880,128]{3,2,1,0:T(8,128)(2,1)S(1)}, bf16[1,1,880,128]{3,2,1,0:T(8,128)(2,1)S(1)}, u32[]{:S(2)}, u32[]{:S(2)}) collective-permute-start(bf16[1,1,880,128]{3,2,1,0:T(8,128)(2,1)S(1)} %slice_bitcast_fusion), channel_id=1, source_target_pairs={{0,16},{1,17},{2,18},{3,19},{4,20},{5,21},{6,22},{7,23},{8,24},{9,... | collective-permute-start | bytes 675848 | tf_op jit(solution)/shard_map/ppermute | solution.py:77
  16.3 12.3 %collective-permute-start.5 = (bf16[1,1,864,128]{3,2,1,0:T(8,128)(2,1)S(1)}, bf16[1,1,864,128]{3,2,1,0:T(8,128)(2,1)S(1)}, u32[]{:S(2)}, u32[]{:S(2)}) collective-permute-start(bf16[1,1,864,128]{3,2,1,0:T(8,128)(2,1)S(1)} %fusion.39), channel_id=1, source_target_pairs={{0,16},{1,17},{2,18},{3,19},{4,20},{5,21},{6,22},{7,23},{8,24},{9,... | collective-permute-start | bytes 663560 | tf_op jit(solution)/shard_map/ppermute | solution.py:77
  16.4 18.3 %collective-permute-start.1 = (bf16[2,1,880,128]{3,2,1,0:T(8,128)(2,1)S(1)}, bf16[2,1,880,128]{3,2,1,0:T(8,128)(2,1)S(1)}, u32[]{:S(2)}, u32[]{:S(2)}) collective-permute-start(bf16[2,1,880,128]{3,2,1,0:T(8,128)(2,1)S(1)} %pad_maximum_fusion.13), channel_id=1, source_target_pairs={{0,8},{1,9},{2,10},{3,11},{4,12},{5,13},{6,14},{7,15},{8,0},{9,1},... | collective-permute-start | bytes 1351688 | tf_op jit(solution)/shard_map/ppermute | solution.py:77
  28.7 14.6 %collective-permute-start.6 = (bf16[2,1,864,128]{3,2,1,0:T(8,128)(2,1)S(1)}, bf16[2,1,864,128]{3,2,1,0:T(8,128)(2,1)S(1)}, u32[]{:S(2)}, u32[]{:S(2)}) collective-permute-start(bf16[2,1,864,128]{3,2,1,0:T(8,128)(2,1)S(1)} %constant_dynamic-update-slice_fusion), channel_id=1, source_target_pairs={{0,8},{1,9},{2,10},{3,11},{4,12},{5,13},{6,14},{7,15},{8,0},{9,1},... | collective-permute-start | bytes 1327112 | tf_op jit(solution)/shard_map/ppermute | solution.py:77
  34.9 9.9 %collective-permute-start.16 = (bf16[1,1,880,128]{3,2,1,0:T(8,128)(2,1)S(1)}, bf16[1,1,880,128]{3,2,1,0:T(8,128)(2,1)S(1)}, u32[]{:S(2)}, u32[]{:S(2)}) collective-permute-start(bf16[1,1,880,128]{3,2,1,0:T(8,128)(2,1)S(1)} %get-tuple-element.140), channel_id=1, source_target_pairs={{0,2},{1,3},{2,0},{3,1},{4,6},{5,7},{6,4},{7,5},{8,10},{9,11},{10,... | collective-permute-start | bytes 675848 | tf_op jit(solution)/shard_map/ppermute | solution.py:77
  36.3 11.9 %collective-permute-start.22 = (bf16[1,1,880,128]{3,2,1,0:T(8,128)(2,1)S(1)}, bf16[1,1,880,128]{3,2,1,0:T(8,128)(2,1)S(1)}, u32[]{:S(2)}, u32[]{:S(2)}) collective-permute-start(bf16[1,1,880,128]{3,2,1,0:T(8,128)(2,1)S(1)} %get-tuple-element.139), channel_id=1, source_target_pairs={{0,2},{1,3},{2,0},{3,1},{4,6},{5,7},{6,4},{7,5},{8,10},{9,11},{10,... | collective-permute-start | bytes 675848 | tf_op jit(solution)/shard_map/ppermute | solution.py:77
  37.0 15.7 %collective-permute-start.10 = (bf16[1,1,880,128]{3,2,1,0:T(8,128)(2,1)S(1)}, bf16[1,1,880,128]{3,2,1,0:T(8,128)(2,1)S(1)}, u32[]{:S(2)}, u32[]{:S(2)}) collective-permute-start(bf16[1,1,880,128]{3,2,1,0:T(8,128)(2,1)S(1)} %get-tuple-element.141), channel_id=1, source_target_pairs={{0,2},{1,3},{2,0},{3,1},{4,6},{5,7},{6,4},{7,5},{8,10},{9,11},{10,... | collective-permute-start | bytes 675848 | tf_op jit(solution)/shard_map/ppermute | solution.py:77
  38.3 16.8 %collective-permute-start.2 = (bf16[1,1,880,128]{3,2,1,0:T(8,128)(2,1)S(1)}, bf16[1,1,880,128]{3,2,1,0:T(8,128)(2,1)S(1)}, u32[]{:S(2)}, u32[]{:S(2)}) collective-permute-start(bf16[1,1,880,128]{3,2,1,0:T(8,128)(2,1)S(1)} %get-tuple-element.142), channel_id=1, source_target_pairs={{0,2},{1,3},{2,0},{3,1},{4,6},{5,7},{6,4},{7,5},{8,10},{9,11},{10,... | collective-permute-start | bytes 675848 | tf_op jit(solution)/shard_map/ppermute | solution.py:77
  43.4 19.2 %collective-permute-start.25 = (bf16[1,1,864,128]{3,2,1,0:T(8,128)(2,1)S(1)}, bf16[1,1,864,128]{3,2,1,0:T(8,128)(2,1)S(1)}, u32[]{:S(2)}, u32[]{:S(2)}) collective-permute-start(bf16[1,1,864,128]{3,2,1,0:T(8,128)(2,1)S(1)} %get-tuple-element.144), channel_id=1, source_target_pairs={{0,4},{1,5},{2,6},{3,7},{4,0},{5,1},{6,2},{7,3},{8,12},{9,13},{10,... | collective-permute-start | bytes 663560 | tf_op jit(solution)/shard_map/ppermute | solution.py:77
  44.8 11.7 %collective-permute-start.19 = (bf16[1,1,864,128]{3,2,1,0:T(8,128)(2,1)S(1)}, bf16[1,1,864,128]{3,2,1,0:T(8,128)(2,1)S(1)}, u32[]{:S(2)}, u32[]{:S(2)}) collective-permute-start(bf16[1,1,864,128]{3,2,1,0:T(8,128)(2,1)S(1)} %get-tuple-element.145), channel_id=1, source_target_pairs={{0,4},{1,5},{2,6},{3,7},{4,0},{5,1},{6,2},{7,3},{8,12},{9,13},{10,... | collective-permute-start | bytes 663560 | tf_op jit(solution)/shard_map/ppermute | solution.py:77
  48.2 13.1 %collective-permute-start.13 = (bf16[1,1,864,128]{3,2,1,0:T(8,128)(2,1)S(1)}, bf16[1,1,864,128]{3,2,1,0:T(8,128)(2,1)S(1)}, u32[]{:S(2)}, u32[]{:S(2)}) collective-permute-start(bf16[1,1,864,128]{3,2,1,0:T(8,128)(2,1)S(1)} %get-tuple-element.146), channel_id=1, source_target_pairs={{0,4},{1,5},{2,6},{3,7},{4,0},{5,1},{6,2},{7,3},{8,12},{9,13},{10,... | collective-permute-start | bytes 663560 | tf_op jit(solution)/shard_map/ppermute | solution.py:77
  52.7 18.3 %collective-permute-start.17 = (bf16[1,2,880,128]{3,2,1,0:T(8,128)(2,1)S(1)}, bf16[1,2,880,128]{3,2,1,0:T(8,128)(2,1)S(1)}, u32[]{:S(2)}, u32[]{:S(2)}) collective-permute-start(bf16[1,2,880,128]{3,2,1,0:T(8,128)(2,1)S(1)} %pad_maximum_fusion.16), channel_id=1, source_target_pairs={{0,4},{1,5},{2,6},{3,7},{4,0},{5,1},{6,2},{7,3},{8,12},{9,13},{10,... | collective-permute-start | bytes 1351688 | tf_op jit(solution)/shard_map/ppermute | solution.py:77
  55.1 31.5 %collective-permute-start.11 = (bf16[1,2,880,128]{3,2,1,0:T(8,128)(2,1)S(1)}, bf16[1,2,880,128]{3,2,1,0:T(8,128)(2,1)S(1)}, u32[]{:S(2)}, u32[]{:S(2)}) collective-permute-start(bf16[1,2,880,128]{3,2,1,0:T(8,128)(2,1)S(1)} %pad_maximum_fusion.15), channel_id=1, source_target_pairs={{0,4},{1,5},{2,6},{3,7},{4,0},{5,1},{6,2},{7,3},{8,12},{9,13},{10,... | collective-permute-start | bytes 1351688 | tf_op jit(solution)/shard_map/ppermute | solution.py:77
  56.5 28.8 %collective-permute-start.7 = (bf16[1,1,864,128]{3,2,1,0:T(8,128)(2,1)S(1)}, bf16[1,1,864,128]{3,2,1,0:T(8,128)(2,1)S(1)}, u32[]{:S(2)}, u32[]{:S(2)}) collective-permute-start(bf16[1,1,864,128]{3,2,1,0:T(8,128)(2,1)S(1)} %get-tuple-element.147), channel_id=1, source_target_pairs={{0,4},{1,5},{2,6},{3,7},{4,0},{5,1},{6,2},{7,3},{8,12},{9,13},{10,... | collective-permute-start | bytes 663560 | tf_op jit(solution)/shard_map/ppermute | solution.py:77
  61.3 33.7 %collective-permute-start.23 = (bf16[1,2,880,128]{3,2,1,0:T(8,128)(2,1)S(1)}, bf16[1,2,880,128]{3,2,1,0:T(8,128)(2,1)S(1)}, u32[]{:S(2)}, u32[]{:S(2)}) collective-permute-start(bf16[1,2,880,128]{3,2,1,0:T(8,128)(2,1)S(1)} %pad_maximum_fusion.17), channel_id=1, source_target_pairs={{0,4},{1,5},{2,6},{3,7},{4,0},{5,1},{6,2},{7,3},{8,12},{9,13},{10,... | collective-permute-start | bytes 1351688 | tf_op jit(solution)/shard_map/ppermute | solution.py:77
  62.6 40.2 %collective-permute-start.3 = (bf16[1,2,880,128]{3,2,1,0:T(8,128)(2,1)S(1)}, bf16[1,2,880,128]{3,2,1,0:T(8,128)(2,1)S(1)}, u32[]{:S(2)}, u32[]{:S(2)}) collective-permute-start(bf16[1,2,880,128]{3,2,1,0:T(8,128)(2,1)S(1)} %pad_maximum_fusion.14), channel_id=1, source_target_pairs={{0,4},{1,5},{2,6},{3,7},{4,0},{5,1},{6,2},{7,3},{8,12},{9,13},{10,... | collective-permute-start | bytes 1351688 | tf_op jit(solution)/shard_map/ppermute | solution.py:77
  70.9 33.2 %collective-permute-start.14 = (bf16[2,1,864,128]{3,2,1,0:T(8,128)(2,1)S(1)}, bf16[2,1,864,128]{3,2,1,0:T(8,128)(2,1)S(1)}, u32[]{:S(2)}, u32[]{:S(2)}) collective-permute-start(bf16[2,1,864,128]{3,2,1,0:T(8,128)(2,1)S(1)} %pad_maximum_fusion.19), channel_id=1, source_target_pairs={{0,2},{1,3},{2,0},{3,1},{4,6},{5,7},{6,4},{7,5},{8,10},{9,11},{10,... | collective-permute-start | bytes 1327112 | tf_op jit(solution)/shard_map/ppermute | solution.py:77
  72.3 32.6 %copy-start = (bf16[2,2,880,128]{3,2,1,0:T(8,128)(2,1)}, bf16[2,2,880,128]{3,2,1,0:T(8,128)(2,1)S(1)}, u32[]{:S(2)}) copy-start(bf16[2,2,880,128]{3,2,1,0:T(8,128)(2,1)S(1)} %pad_maximum_fusion.3) | copy-start | bytes 2703364
  85.3 19.7 %collective-permute-start.20 = (bf16[2,1,864,128]{3,2,1,0:T(8,128)(2,1)S(1)}, bf16[2,1,864,128]{3,2,1,0:T(8,128)(2,1)S(1)}, u32[]{:S(2)}, u32[]{:S(2)}) collective-permute-start(bf16[2,1,864,128]{3,2,1,0:T(8,128)(2,1)S(1)} %pad_maximum_fusion.20), channel_id=1, source_target_pairs={{0,2},{1,3},{2,0},{3,1},{4,6},{5,7},{6,4},{7,5},{8,10},{9,11},{10,... | collective-permute-start | bytes 1327112 | tf_op jit(solution)/shard_map/ppermute | solution.py:77
  86.6 37.1 %collective-permute-start.18 = (bf16[2,2,880,128]{3,2,1,0:T(8,128)(2,1)S(1)}, bf16[2,2,880,128]{3,2,1,0:T(8,128)(2,1)S(1)}, u32[]{:S(2)}, u32[]{:S(2)}) collective-permute-start(bf16[2,2,880,128]{3,2,1,0:T(8,128)(2,1)S(1)} %pad_maximum_fusion.3), channel_id=1, source_target_pairs={{0,1},{1,0},{2,3},{3,2},{4,5},{5,4},{6,7},{7,6},{8,9},{9,8},{10,11... | collective-permute-start | bytes 2703368 | tf_op jit(solution)/shard_map/ppermute | solution.py:77
  86.8 19.5 %copy-start.1 = (bf16[2,2,880,128]{3,2,1,0:T(8,128)(2,1)}, bf16[2,2,880,128]{3,2,1,0:T(8,128)(2,1)S(1)}, u32[]{:S(2)}) copy-start(bf16[2,2,880,128]{3,2,1,0:T(8,128)(2,1)S(1)} %pad_maximum_fusion.2) | copy-start | bytes 2703364
  95.0 29.4 %collective-permute-start.12 = (bf16[2,2,880,128]{3,2,1,0:T(8,128)(2,1)S(1)}, bf16[2,2,880,128]{3,2,1,0:T(8,128)(2,1)S(1)}, u32[]{:S(2)}, u32[]{:S(2)}) collective-permute-start(bf16[2,2,880,128]{3,2,1,0:T(8,128)(2,1)S(1)} %pad_maximum_fusion.2), channel_id=1, source_target_pairs={{0,1},{1,0},{2,3},{3,2},{4,5},{5,4},{6,7},{7,6},{8,9},{9,8},{10,11... | collective-permute-start | bytes 2703368 | tf_op jit(solution)/shard_map/ppermute | solution.py:77
  102.8 13.0 %collective-permute-start.26 = (bf16[2,1,864,128]{3,2,1,0:T(8,128)(2,1)S(1)}, bf16[2,1,864,128]{3,2,1,0:T(8,128)(2,1)S(1)}, u32[]{:S(2)}, u32[]{:S(2)}) collective-permute-start(bf16[2,1,864,128]{3,2,1,0:T(8,128)(2,1)S(1)} %pad_maximum_fusion.21), channel_id=1, source_target_pairs={{0,2},{1,3},{2,0},{3,1},{4,6},{5,7},{6,4},{7,5},{8,10},{9,11},{10,... | collective-permute-start | bytes 1327112 | tf_op jit(solution)/shard_map/ppermute | solution.py:77
  104.1 18.6 %collective-permute-start.8 = (bf16[2,1,864,128]{3,2,1,0:T(8,128)(2,1)S(1)}, bf16[2,1,864,128]{3,2,1,0:T(8,128)(2,1)S(1)}, u32[]{:S(2)}, u32[]{:S(2)}) collective-permute-start(bf16[2,1,864,128]{3,2,1,0:T(8,128)(2,1)S(1)} %pad_maximum_fusion.18), channel_id=1, source_target_pairs={{0,2},{1,3},{2,0},{3,1},{4,6},{5,7},{6,4},{7,5},{8,10},{9,11},{10,... | collective-permute-start | bytes 1327112 | tf_op jit(solution)/shard_map/ppermute | solution.py:77
  105.0 18.7 %copy-start.3 = (bf16[2,2,864,128]{3,2,1,0:T(8,128)(2,1)}, bf16[2,2,864,128]{3,2,1,0:T(8,128)(2,1)S(1)}, u32[]{:S(2)}) copy-start(bf16[2,2,864,128]{3,2,1,0:T(8,128)(2,1)S(1)} %pad_maximum_fusion.9) | copy-start | bytes 2654212
  105.0 19.6 %collective-permute-start.15 = (bf16[2,2,864,128]{3,2,1,0:T(8,128)(2,1)S(1)}, bf16[2,2,864,128]{3,2,1,0:T(8,128)(2,1)S(1)}, u32[]{:S(2)}, u32[]{:S(2)}) collective-permute-start(bf16[2,2,864,128]{3,2,1,0:T(8,128)(2,1)S(1)} %pad_maximum_fusion.9), channel_id=1, source_target_pairs={{0,1},{1,0},{2,3},{3,2},{4,5},{5,4},{6,7},{7,6},{8,9},{9,8},{10,11... | collective-permute-start | bytes 2654216 | tf_op jit(solution)/shard_map/ppermute | solution.py:77
  106.3 18.3 %copy-start.2 = (bf16[2,2,864,128]{3,2,1,0:T(8,128)(2,1)}, bf16[2,2,864,128]{3,2,1,0:T(8,128)(2,1)S(1)}, u32[]{:S(2)}) copy-start(bf16[2,2,864,128]{3,2,1,0:T(8,128)(2,1)S(1)} %pad_maximum_fusion.10) | copy-start | bytes 2654212
  115.9 25.1 %collective-permute-start.4 = (bf16[2,2,880,128]{3,2,1,0:T(8,128)(2,1)}, bf16[2,2,880,128]{3,2,1,0:T(8,128)(2,1)}, u32[]{:S(2)}, u32[]{:S(2)}) collective-permute-start(bf16[2,2,880,128]{3,2,1,0:T(8,128)(2,1)} %pad_maximum_fusion.1), channel_id=1, source_target_pairs={{0,1},{1,0},{2,3},{3,2},{4,5},{5,4},{6,7},{7,6},{8,9},{9,8},{10,11... | collective-permute-start | bytes 2703368 | tf_op jit(solution)/shard_map/ppermute | solution.py:77
  122.7 10.7 %collective-permute-start.21 = (bf16[2,2,864,128]{3,2,1,0:T(8,128)(2,1)S(1)}, bf16[2,2,864,128]{3,2,1,0:T(8,128)(2,1)}, u32[]{:S(2)}, u32[]{:S(2)}) collective-permute-start(bf16[2,2,864,128]{3,2,1,0:T(8,128)(2,1)S(1)} %pad_maximum_fusion.10), channel_id=1, source_target_pairs={{0,1},{1,0},{2,3},{3,2},{4,5},{5,4},{6,7},{7,6},{8,9},{9,8},{10,11... | collective-permute-start | bytes 2654216 | tf_op jit(solution)/shard_map/ppermute | solution.py:77
  123.7 17.3 %collective-permute-start.9 = (bf16[2,2,864,128]{3,2,1,0:T(8,128)(2,1)}, bf16[2,2,864,128]{3,2,1,0:T(8,128)(2,1)}, u32[]{:S(2)}, u32[]{:S(2)}) collective-permute-start(bf16[2,2,864,128]{3,2,1,0:T(8,128)(2,1)} %pad_maximum_fusion.8), channel_id=1, source_target_pairs={{0,1},{1,0},{2,3},{3,2},{4,5},{5,4},{6,7},{7,6},{8,9},{9,8},{10,11... | collective-permute-start | bytes 2654216 | tf_op jit(solution)/shard_map/ppermute | solution.py:77
  124.4 63.9 %collective-permute-start.24 = (bf16[2,2,880,128]{3,2,1,0:T(8,128)(2,1)S(1)}, bf16[2,2,880,128]{3,2,1,0:T(8,128)(2,1)}, u32[]{:S(2)}, u32[]{:S(2)}) collective-permute-start(bf16[2,2,880,128]{3,2,1,0:T(8,128)(2,1)S(1)} %pad_maximum_fusion.4), channel_id=1, source_target_pairs={{0,1},{1,0},{2,3},{3,2},{4,5},{5,4},{6,7},{7,6},{8,9},{9,8},{10,11... | collective-permute-start | bytes 2703368 | tf_op jit(solution)/shard_map/ppermute | solution.py:77
  124.6 5.1 %copy-start.8 = (bf16[2,2,864,128]{3,2,1,0:T(8,128)(2,1)}, bf16[2,2,864,128]{3,2,1,0:T(8,128)(2,1)S(1)}, u32[]{:S(2)}) copy-start(bf16[2,2,864,128]{3,2,1,0:T(8,128)(2,1)S(1)} %pad_maximum_fusion.11) | copy-start | bytes 2654212
  126.3 62.0 %collective-permute-start.27 = (bf16[2,2,864,128]{3,2,1,0:T(8,128)(2,1)S(1)}, bf16[2,2,864,128]{3,2,1,0:T(8,128)(2,1)S(1)}, u32[]{:S(2)}, u32[]{:S(2)}) collective-permute-start(bf16[2,2,864,128]{3,2,1,0:T(8,128)(2,1)S(1)} %pad_maximum_fusion.11), channel_id=1, source_target_pairs={{0,1},{1,0},{2,3},{3,2},{4,5},{5,4},{6,7},{7,6},{8,9},{9,8},{10,11... | collective-permute-start | bytes 2654216 | tf_op jit(solution)/shard_map/ppermute | solution.py:77
  275.8 6.8 %collective-permute-start.42 = (bf16[2,2,864,128]{3,2,1,0:T(8,128)(2,1)S(1)}, bf16[2,2,864,128]{3,2,1,0:T(8,128)(2,1)S(1)}, u32[]{:S(2)}, u32[]{:S(2)}) collective-permute-start(bf16[2,2,864,128]{3,2,1,0:T(8,128)(2,1)S(1)} %dynamic-slice_bitcast_fusion.4), channel_id=1, source_target_pairs={{0,1},{1,0},{2,3},{3,2},{4,5},{5,4},{6,7},{7,6},{8,9},{9,8},{10,11... | collective-permute-start | bytes 2654216 | tf_op jit(solution)/shard_map/ppermute | solution.py:77
  277.4 9.4 %collective-permute-start.28 = (bf16[2,2,880,128]{3,2,1,0:T(8,128)(2,1)S(1)}, bf16[2,2,880,128]{3,2,1,0:T(8,128)(2,1)S(1)}, u32[]{:S(2)}, u32[]{:S(2)}) collective-permute-start(bf16[2,2,880,128]{3,2,1,0:T(8,128)(2,1)S(1)} %dynamic-slice_bitcast_fusion.3), channel_id=1, source_target_pairs={{0,1},{1,0},{2,3},{3,2},{4,5},{5,4},{6,7},{7,6},{8,9},{9,8},{10,11... | collective-permute-start | bytes 2703368 | tf_op jit(solution)/shard_map/ppermute | solution.py:77
  277.9 6.0 %collective-permute-start.45 = (bf16[2,2,864,128]{3,2,0,1:T(8,128)(2,1)S(1)}, bf16[2,2,864,128]{3,2,0,1:T(8,128)(2,1)S(1)}, u32[]{:S(2)}, u32[]{:S(2)}) collective-permute-start(bf16[2,2,864,128]{3,2,0,1:T(8,128)(2,1)S(1)} %bitcast.288), channel_id=1, source_target_pairs={{0,1},{1,0},{2,3},{3,2},{4,5},{5,4},{6,7},{7,6},{8,9},{9,8},{10,11... | collective-permute-start | bytes 2654216 | tf_op jit(solution)/shard_map/ppermute | solution.py:77
  279.2 9.0 %collective-permute-start.31 = (bf16[2,2,880,128]{3,2,1,0:T(8,128)(2,1)S(1)}, bf16[2,2,880,128]{3,2,1,0:T(8,128)(2,1)S(1)}, u32[]{:S(2)}, u32[]{:S(2)}) collective-permute-start(bf16[2,2,880,128]{3,2,1,0:T(8,128)(2,1)S(1)} %dynamic-slice_bitcast_fusion.2), channel_id=1, source_target_pairs={{0,1},{1,0},{2,3},{3,2},{4,5},{5,4},{6,7},{7,6},{8,9},{9,8},{10,11... | collective-permute-start | bytes 2703368 | tf_op jit(solution)/shard_map/ppermute | solution.py:77
  280.6 4.0 %collective-permute-start.48 = (bf16[2,2,864,128]{3,2,0,1:T(8,128)(2,1)S(1)}, bf16[2,2,864,128]{3,2,0,1:T(8,128)(2,1)S(1)}, u32[]{:S(2)}, u32[]{:S(2)}) collective-permute-start(bf16[2,2,864,128]{3,2,0,1:T(8,128)(2,1)S(1)} %bitcast.290), channel_id=1, source_target_pairs={{0,1},{1,0},{2,3},{3,2},{4,5},{5,4},{6,7},{7,6},{8,9},{9,8},{10,11... | collective-permute-start | bytes 2654216 | tf_op jit(solution)/shard_map/ppermute | solution.py:77
  282.6 2.5 collective-permute-start.51
  283.9 5.6 %collective-permute-start.34 = (bf16[2,2,880,128]{3,2,1,0:T(8,128)(2,1)S(1)}, bf16[2,2,880,128]{3,2,1,0:T(8,128)(2,1)S(1)}, u32[]{:S(2)}, u32[]{:S(2)}) collective-permute-start(bf16[2,2,880,128]{3,2,1,0:T(8,128)(2,1)S(1)} %dynamic-slice_bitcast_fusion.1), channel_id=1, source_target_pairs={{0,1},{1,0},{2,3},{3,2},{4,5},{5,4},{6,7},{7,6},{8,9},{9,8},{10,11... | collective-permute-start | bytes 2703368 | tf_op jit(solution)/shard_map/ppermute | solution.py:77
  284.6 6.3 %collective-permute-start.37 = (bf16[2,2,880,128]{3,2,1,0:T(8,128)(2,1)S(1)}, bf16[2,2,880,128]{3,2,1,0:T(8,128)(2,1)S(1)}, u32[]{:S(2)}, u32[]{:S(2)}) collective-permute-start(bf16[2,2,880,128]{3,2,1,0:T(8,128)(2,1)S(1)} %dynamic-slice_bitcast_fusion), channel_id=1, source_target_pairs={{0,1},{1,0},{2,3},{3,2},{4,5},{5,4},{6,7},{7,6},{8,9},{9,8},{10,11... | collective-permute-start | bytes 2703368 | tf_op jit(solution)/shard_map/ppermute | solution.py:77
  285.1 13.1 %collective-permute-start.43 = (bf16[2,864,128]{2,1,0:T(8,128)(2,1)S(1)}, bf16[2,864,128]{2,1,0:T(8,128)(2,1)S(1)}, u32[]{:S(2)}, u32[]{:S(2)}) collective-permute-start(bf16[2,864,128]{2,1,0:T(8,128)(2,1)S(1)} %dynamic-slice_bitcast_fusion.14), channel_id=1, source_target_pairs={{0,2},{1,3},{2,0},{3,1},{4,6},{5,7},{6,4},{7,5},{8,10},{9,11},{10,... | collective-permute-start | bytes 1327112 | tf_op jit(solution)/shard_map/ppermute | solution.py:77
  286.8 20.9 %collective-permute-start.46 = (bf16[2,864,128]{2,1,0:T(8,128)(2,1)S(1)}, bf16[2,864,128]{2,1,0:T(8,128)(2,1)S(1)}, u32[]{:S(2)}, u32[]{:S(2)}) collective-permute-start(bf16[2,864,128]{2,1,0:T(8,128)(2,1)S(1)} %dynamic-slice_bitcast_fusion.13), channel_id=1, source_target_pairs={{0,2},{1,3},{2,0},{3,1},{4,6},{5,7},{6,4},{7,5},{8,10},{9,11},{10,... | collective-permute-start | bytes 1327112 | tf_op jit(solution)/shard_map/ppermute | solution.py:77
  288.2 28.9 %collective-permute-start.49 = (bf16[2,864,128]{2,1,0:T(8,128)(2,1)S(1)}, bf16[2,864,128]{2,1,0:T(8,128)(2,1)S(1)}, u32[]{:S(2)}, u32[]{:S(2)}) collective-permute-start(bf16[2,864,128]{2,1,0:T(8,128)(2,1)S(1)} %dynamic-slice_bitcast_fusion.12), channel_id=1, source_target_pairs={{0,2},{1,3},{2,0},{3,1},{4,6},{5,7},{6,4},{7,5},{8,10},{9,11},{10,... | collective-permute-start | bytes 1327112 | tf_op jit(solution)/shard_map/ppermute | solution.py:77
  289.5 36.5 %collective-permute-start.52 = (bf16[2,864,128]{2,1,0:T(8,128)(2,1)S(1)}, bf16[2,864,128]{2,1,0:T(8,128)(2,1)S(1)}, u32[]{:S(2)}, u32[]{:S(2)}) collective-permute-start(bf16[2,864,128]{2,1,0:T(8,128)(2,1)S(1)} %dynamic-slice_bitcast_fusion.11), channel_id=1, source_target_pairs={{0,2},{1,3},{2,0},{3,1},{4,6},{5,7},{6,4},{7,5},{8,10},{9,11},{10,... | collective-permute-start | bytes 1327112 | tf_op jit(solution)/shard_map/ppermute | solution.py:77
  290.9 36.6 %collective-permute-start.29 = (bf16[2,880,128]{2,1,0:T(8,128)(2,1)S(1)}, bf16[2,880,128]{2,1,0:T(8,128)(2,1)S(1)}, u32[]{:S(2)}, u32[]{:S(2)}) collective-permute-start(bf16[2,880,128]{2,1,0:T(8,128)(2,1)S(1)} %dynamic-slice_bitcast_fusion.9), channel_id=1, source_target_pairs={{0,4},{1,5},{2,6},{3,7},{4,0},{5,1},{6,2},{7,3},{8,12},{9,13},{10,... | collective-permute-start | bytes 1351688 | tf_op jit(solution)/shard_map/ppermute | solution.py:77
  298.2 30.2 %collective-permute-start.32 = (bf16[2,880,128]{2,1,0:T(8,128)(2,1)S(1)}, bf16[2,880,128]{2,1,0:T(8,128)(2,1)S(1)}, u32[]{:S(2)}, u32[]{:S(2)}) collective-permute-start(bf16[2,880,128]{2,1,0:T(8,128)(2,1)S(1)} %dynamic-slice_bitcast_fusion.8), channel_id=1, source_target_pairs={{0,4},{1,5},{2,6},{3,7},{4,0},{5,1},{6,2},{7,3},{8,12},{9,13},{10,... | collective-permute-start | bytes 1351688 | tf_op jit(solution)/shard_map/ppermute | solution.py:77
  307.7 22.3 %collective-permute-start.35 = (bf16[2,880,128]{2,1,0:T(8,128)(2,1)S(1)}, bf16[2,880,128]{2,1,0:T(8,128)(2,1)S(1)}, u32[]{:S(2)}, u32[]{:S(2)}) collective-permute-start(bf16[2,880,128]{2,1,0:T(8,128)(2,1)S(1)} %dynamic-slice_bitcast_fusion.7), channel_id=1, source_target_pairs={{0,4},{1,5},{2,6},{3,7},{4,0},{5,1},{6,2},{7,3},{8,12},{9,13},{10,... | collective-permute-start | bytes 1351688 | tf_op jit(solution)/shard_map/ppermute | solution.py:77
  317.1 16.0 %collective-permute-start.38 = (bf16[2,880,128]{2,1,0:T(8,128)(2,1)S(1)}, bf16[2,880,128]{2,1,0:T(8,128)(2,1)S(1)}, u32[]{:S(2)}, u32[]{:S(2)}) collective-permute-start(bf16[2,880,128]{2,1,0:T(8,128)(2,1)S(1)} %dynamic-slice_bitcast_fusion.6), channel_id=1, source_target_pairs={{0,4},{1,5},{2,6},{3,7},{4,0},{5,1},{6,2},{7,3},{8,12},{9,13},{10,... | collective-permute-start | bytes 1351688 | tf_op jit(solution)/shard_map/ppermute | solution.py:77
  326.0 11.9 %collective-permute-start.44 = (bf16[864,128]{1,0:T(8,128)(2,1)S(1)}, bf16[864,128]{1,0:T(8,128)(2,1)S(1)}, u32[]{:S(2)}, u32[]{:S(2)}) collective-permute-start(bf16[864,128]{1,0:T(8,128)(2,1)S(1)} %dynamic-slice_bitcast_fusion.28), channel_id=1, source_target_pairs={{0,4},{1,5},{2,6},{3,7},{4,0},{5,1},{6,2},{7,3},{8,12},{9,13},{10,... | collective-permute-start | bytes 663560 | tf_op jit(solution)/shard_map/ppermute | solution.py:77
  327.5 15.1 %collective-permute-start.47 = (bf16[864,128]{1,0:T(8,128)(2,1)S(1)}, bf16[864,128]{1,0:T(8,128)(2,1)S(1)}, u32[]{:S(2)}, u32[]{:S(2)}) collective-permute-start(bf16[864,128]{1,0:T(8,128)(2,1)S(1)} %dynamic-slice_bitcast_fusion.27), channel_id=1, source_target_pairs={{0,4},{1,5},{2,6},{3,7},{4,0},{5,1},{6,2},{7,3},{8,12},{9,13},{10,... | collective-permute-start | bytes 663560 | tf_op jit(solution)/shard_map/ppermute | solution.py:77
  328.4 18.9 %collective-permute-start.50 = (bf16[864,128]{1,0:T(8,128)(2,1)S(1)}, bf16[864,128]{1,0:T(8,128)(2,1)S(1)}, u32[]{:S(2)}, u32[]{:S(2)}) collective-permute-start(bf16[864,128]{1,0:T(8,128)(2,1)S(1)} %dynamic-slice_bitcast_fusion.26), channel_id=1, source_target_pairs={{0,4},{1,5},{2,6},{3,7},{4,0},{5,1},{6,2},{7,3},{8,12},{9,13},{10,... | collective-permute-start | bytes 663560 | tf_op jit(solution)/shard_map/ppermute | solution.py:77
  330.0 20.6 %collective-permute-start.53 = (bf16[864,128]{1,0:T(8,128)(2,1)S(1)}, bf16[864,128]{1,0:T(8,128)(2,1)S(1)}, u32[]{:S(2)}, u32[]{:S(2)}) collective-permute-start(bf16[864,128]{1,0:T(8,128)(2,1)S(1)} %dynamic-slice_bitcast_fusion.25), channel_id=1, source_target_pairs={{0,4},{1,5},{2,6},{3,7},{4,0},{5,1},{6,2},{7,3},{8,12},{9,13},{10,... | collective-permute-start | bytes 663560 | tf_op jit(solution)/shard_map/ppermute | solution.py:77
  333.1 18.5 %collective-permute-start.30 = (bf16[880,128]{1,0:T(8,128)(2,1)S(1)}, bf16[880,128]{1,0:T(8,128)(2,1)S(1)}, u32[]{:S(2)}, u32[]{:S(2)}) collective-permute-start(bf16[880,128]{1,0:T(8,128)(2,1)S(1)} %dynamic-slice_bitcast_fusion.19), channel_id=1, source_target_pairs={{0,2},{1,3},{2,0},{3,1},{4,6},{5,7},{6,4},{7,5},{8,10},{9,11},{10,... | collective-permute-start | bytes 675848 | tf_op jit(solution)/shard_map/ppermute | solution.py:77
  337.9 13.8 %collective-permute-start.33 = (bf16[880,128]{1,0:T(8,128)(2,1)S(1)}, bf16[880,128]{1,0:T(8,128)(2,1)S(1)}, u32[]{:S(2)}, u32[]{:S(2)}) collective-permute-start(bf16[880,128]{1,0:T(8,128)(2,1)S(1)} %dynamic-slice_bitcast_fusion.18), channel_id=1, source_target_pairs={{0,2},{1,3},{2,0},{3,1},{4,6},{5,7},{6,4},{7,5},{8,10},{9,11},{10,... | collective-permute-start | bytes 675848 | tf_op jit(solution)/shard_map/ppermute | solution.py:77
  342.6 9.1 %collective-permute-start.36 = (bf16[880,128]{1,0:T(8,128)(2,1)S(1)}, bf16[880,128]{1,0:T(8,128)(2,1)S(1)}, u32[]{:S(2)}, u32[]{:S(2)}) collective-permute-start(bf16[880,128]{1,0:T(8,128)(2,1)S(1)} %dynamic-slice_bitcast_fusion.17), channel_id=1, source_target_pairs={{0,2},{1,3},{2,0},{3,1},{4,6},{5,7},{6,4},{7,5},{8,10},{9,11},{10,... | collective-permute-start | bytes 675848 | tf_op jit(solution)/shard_map/ppermute | solution.py:77
  347.3 6.2 %collective-permute-start.39 = (bf16[880,128]{1,0:T(8,128)(2,1)S(1)}, bf16[880,128]{1,0:T(8,128)(2,1)S(1)}, u32[]{:S(2)}, u32[]{:S(2)}) collective-permute-start(bf16[880,128]{1,0:T(8,128)(2,1)S(1)} %dynamic-slice_bitcast_fusion.16), channel_id=1, source_target_pairs={{0,2},{1,3},{2,0},{3,1},{4,6},{5,7},{6,4},{7,5},{8,10},{9,11},{10,... | collective-permute-start | bytes 675848 | tf_op jit(solution)/shard_map/ppermute | solution.py:77
  351.6 13.4 %collective-permute-start.54 = (bf16[2,864,128]{2,1,0:T(8,128)(2,1)}, bf16[2,864,128]{2,1,0:T(8,128)(2,1)}, u32[]{:S(2)}, u32[]{:S(2)}) collective-permute-start(bf16[2,864,128]{2,1,0:T(8,128)(2,1)} %dynamic-slice_bitcast_fusion.10), channel_id=1, source_target_pairs={{0,8},{1,9},{2,10},{3,11},{4,12},{5,13},{6,14},{7,15},{8,0},{9,1},... | collective-permute-start | bytes 1327112 | tf_op jit(solution)/shard_map/ppermute | solution.py:77
  354.6 22.3 %collective-permute-start.40 = (bf16[2,880,128]{2,1,0:T(8,128)(2,1)}, bf16[2,880,128]{2,1,0:T(8,128)(2,1)S(1)}, u32[]{:S(2)}, u32[]{:S(2)}) collective-permute-start(bf16[2,880,128]{2,1,0:T(8,128)(2,1)} %dynamic-slice_bitcast_fusion.5), channel_id=1, source_target_pairs={{0,8},{1,9},{2,10},{3,11},{4,12},{5,13},{6,14},{7,15},{8,0},{9,1},... | collective-permute-start | bytes 1351688 | tf_op jit(solution)/shard_map/ppermute | solution.py:77
  366.1 22.7 %copy-start.7 = (f32[221568]{0:T(1024)S(1)}, f32[221568]{0:T(1024)}, u32[]{:S(2)}) copy-start(f32[221568]{0:T(1024)} %param.9) | copy-start | bytes 2658820
  366.1 22.7 %copy-start.20 = (f32[221568]{0:T(1024)S(1)}, f32[221568]{0:T(1024)}, u32[]{:S(2)}) copy-start(f32[221568]{0:T(1024)} %param.11) | copy-start | bytes 2658820
  366.1 22.6 %copy-start.21 = (f32[221568]{0:T(1024)S(1)}, f32[221568]{0:T(1024)}, u32[]{:S(2)}) copy-start(f32[221568]{0:T(1024)} %param.10) | copy-start | bytes 2658820
  366.1 11.5 %collective-permute-start.55 = (bf16[864,128]{1,0:T(8,128)(2,1)S(1)}, bf16[864,128]{1,0:T(8,128)(2,1)S(1)}, u32[]{:S(2)}, u32[]{:S(2)}) collective-permute-start(bf16[864,128]{1,0:T(8,128)(2,1)S(1)} %dynamic-slice_bitcast_fusion.24), channel_id=1, source_target_pairs={{0,16},{1,17},{2,18},{3,19},{4,20},{5,21},{6,22},{7,23},{8,24},{9,... | collective-permute-start | bytes 663560 | tf_op jit(solution)/shard_map/ppermute | solution.py:77
  377.0 11.7 %collective-permute-start.41 = (bf16[880,128]{1,0:T(8,128)(2,1)S(1)}, bf16[880,128]{1,0:T(8,128)(2,1)S(1)}, u32[]{:S(2)}, u32[]{:S(2)}) collective-permute-start(bf16[880,128]{1,0:T(8,128)(2,1)S(1)} %dynamic-slice_bitcast_fusion.15), channel_id=1, source_target_pairs={{0,16},{1,17},{2,18},{3,19},{4,20},{5,21},{6,22},{7,23},{8,24},{9,... | collective-permute-start | bytes 675848 | tf_op jit(solution)/shard_map/ppermute | solution.py:77
  (15 other events, 29.7 us)
